TPU v7x, 32 devices: a whole 2x2x4 slice. The times are simulated.
32 devices in a mesh: seq: 4 (over z), wsh: 8 (over y, x, core).
Axes of the slice: x: 2, y: 2, z: 4, core: 2. Of those that a mesh axis runs over, the one named last changes fastest.
Arguments:
- inputs: bfloat16 [8, 1024, 2048], P('wsh', 'seq'), may hold values from -6 to 6
- cotangent: bfloat16 [8, 1024, 2048], P('wsh', 'seq'), may hold values from -6 to 6
- teacher: bfloat16 [8, 1024, 2048], P('wsh', 'seq'), may hold values from -6 to 6
- document_ids: int32 [8, 1024], P('wsh'), may hold values from 0 to 9, never falling along the last dimension, each value on 1 to 512 neighbouring positions
- valid_flags: int32 [8, 1024], P('wsh', 'seq'), may hold values from 0 to 1, as said below
- step_count: int32 [1], replicated, may hold values from 1 to 20
- attn_params: float32 [2048, 8197], P(('seq', 'wsh')), may hold values from -2 to 2
- attn_first: float32 [2048, 8197], P(('seq', 'wsh')), may hold values from -8192 to 8192
- attn_second: float32 [2048, 8197], P(('seq', 'wsh')), may hold values from 0 to 49152, as said below
- mlp_params: float32 [2048, 16391], P(('seq', 'wsh')), may hold values from -2 to 2
- mlp_first: float32 [2048, 16391], P(('seq', 'wsh')), may hold values from -8192 to 8192
- mlp_second: float32 [2048, 16391], P(('seq', 'wsh')), may hold values from 0 to 49152, as said below
Outputs:
- block_output: bfloat16 [8, 1024, 2048], P('wsh', 'seq')
- losses: float32 [1], replicated
- input_grad: float32 [8, 1024, 2048], P('wsh', 'seq')
- vector_gradient: float32 [2048, 12], P(('seq', 'wsh'))
- attn_params_new: float32 [2048, 8197], P(('seq', 'wsh'))
- attn_first_new: float32 [2048, 8197], P(('seq', 'wsh'))
- attn_second_new: float32 [2048, 8197], P(('seq', 'wsh'))
- mlp_params_new: float32 [2048, 16391], P(('seq', 'wsh'))
- mlp_first_new: float32 [2048, 16391], P(('seq', 'wsh'))
- mlp_second_new: float32 [2048, 16391], P(('seq', 'wsh'))
Inputs may be any that keep to these rules, and one draw needn't show every extreme that they name: `document_ids`: document numbers never fall along a sequence; a document has 1 to 512 tokens, and some document has exactly 512. `valid_flags`: in each sequence the valid tokens form a prefix of at least 256 tokens. `attn_second`: every entry is positive. `mlp_second`: every entry is positive.
All inputs are finite; a program needn't handle non-finite values.
Results may differ from a plain program's by a relative error of at most 0.007.
The roundings to bfloat16 on the way count: a program that leaves them out, or rounds other values in their place, can miss the bound.
Values may be sent and summed in bfloat16 or wider, within the bound.
A program may use at most 640 MiB of HBM per device.

v0:
```python
import math

import jax
import jax.numpy as jnp
from jax import lax
from jax.sharding import PartitionSpec as P

D = 2048
H = 16
DH = 128
FF = 8192
QBLK = 512
UPC = 4


eps_norm = 1e-05
beta_one = 0.9
beta_two = 0.95
adam_eps = 1e-08
decay_rate = 0.1
learn_rate = 0.05
gelu_coef = 0.7978845608028654


def layer_norm(value, gain, shift):
    row_mean = jnp.mean(value, axis=-1, keepdims=True)
    centred = value - row_mean
    variance = jnp.mean(centred * centred, axis=-1, keepdims=True)
    return centred * lax.rsqrt(variance + eps_norm) * gain + shift


def gelu_tanh(value):
    return 0.5 * value * (1.0 + jnp.tanh(gelu_coef * (value + 0.044715 * value * value * value)))


def adam_update(weights, first, second, gradient, step_count):
    steps_done = step_count[0].astype(jnp.float32)
    first_new = beta_one * first + (1.0 - beta_one) * gradient
    second_new = beta_two * second + (1.0 - beta_two) * gradient * gradient
    fix_one = 1.0 - jnp.power(beta_one, steps_done)
    fix_two = 1.0 - jnp.power(beta_two, steps_done)
    update = first_new / fix_one / (jnp.sqrt(second_new / fix_two) + adam_eps)
    return (weights - learn_rate * (update + decay_rate * weights), first_new, second_new)


def contract_rows(left, right):
    return lax.dot_general(
        left, right, (((0,), (0,)), ((), ())), preferred_element_type=jnp.float32
    )


def contract_cols(left, right):
    return lax.dot_general(
        left, right, (((1,), (1,)), ((), ())), preferred_element_type=jnp.float32
    )


def block_scores(q_rows, key_rows, row_start, slopes, doc_row, score_scale):
    rows_here = q_rows.shape[0]
    keys_here = key_rows.shape[0]
    scores = (
        jnp.einsum("qhd,khd->hqk", q_rows, key_rows, preferred_element_type=jnp.float32)
        * score_scale
    )
    row_pos = row_start + jnp.arange(rows_here, dtype=jnp.int32)
    key_pos = jnp.arange(keys_here, dtype=jnp.int32)
    distance = (row_pos[:, None] - key_pos[None, :]).astype(jnp.float32)
    scores = scores - slopes[:, None, None] * distance[None]
    doc_rows = doc_row[row_start : row_start + rows_here]
    allowed = (doc_rows[:, None] == doc_row[None, :]) & (key_pos[None, :] <= row_pos[:, None])
    return jnp.where(allowed[None], scores, -jnp.inf)


def shards(
    inputs,
    cotangent,
    teacher,
    document_ids,
    valid_flags,
    step_count,
    attn_params,
    attn_first,
    attn_second,
    mlp_params,
    mlp_first,
    mlp_second,
):
    tok_rows = inputs.shape[1]
    seq_size = lax.axis_size("seq")
    seq_len = tok_rows * seq_size
    token_total = seq_len * lax.axis_size("wsh")
    heads_here = H // seq_size
    head_cols = heads_here * DH
    score_scale = 1.0 / math.sqrt(DH)
    nblocks = seq_len // QBLK
    attn_low = attn_params.astype(jnp.bfloat16)
    mlp_low = mlp_params.astype(jnp.bfloat16)
    attn_full, mlp_full = (
        lax.all_gather(attn_low, ("seq", "wsh"), axis=0, tiled=True),
        lax.all_gather(mlp_low, ("seq", "wsh"), axis=0, tiled=True),
    )
    w_qkv = attn_full[:, : 3 * D]
    w_dense = attn_full[:, 3 * D : 4 * D]
    attn_vectors = attn_full[:, 4 * D :].astype(jnp.float32)
    gain_one = attn_vectors[:, 0]
    shift_one = attn_vectors[:, 1]
    bias_query = attn_vectors[:, 2]
    bias_value = attn_vectors[:, 3]
    bias_dense = attn_vectors[:, 4]
    acts = inputs[0].astype(jnp.float32)
    normed, norm_one_back = jax.vjp(layer_norm, acts, gain_one, shift_one)
    normed_low = normed.astype(jnp.bfloat16)
    qkv_bias = jnp.concatenate([bias_query, jnp.zeros_like(bias_query), bias_value])
    projected = (jnp.dot(normed_low, w_qkv, preferred_element_type=jnp.float32) + qkv_bias).astype(
        jnp.bfloat16
    )
    sent = projected.reshape(tok_rows, 3, seq_size, head_cols)
    arrived = lax.all_to_all(sent, "seq", split_axis=2, concat_axis=0, tiled=True).reshape(
        seq_len, 3, heads_here, DH
    )
    queries = arrived[:, 0]
    keys_all = arrived[:, 1]
    values = arrived[:, 2]
    head_ids = lax.axis_index("seq") * heads_here + jnp.arange(heads_here, dtype=jnp.int32)
    slopes = jnp.exp2(-8.0 * (head_ids.astype(jnp.float32) + 1.0) / H)
    doc_row = document_ids[0]
    out_blocks = []
    log_blocks = []
    for block_index in range(nblocks):
        row_start = block_index * QBLK
        key_end = seq_len
        scores = block_scores(
            queries[row_start : row_start + QBLK], keys_all, row_start, slopes, doc_row, score_scale
        )
        row_top = jnp.max(scores, axis=-1, keepdims=True)
        exp_scores = jnp.exp(scores - row_top)
        row_total = jnp.sum(exp_scores, axis=-1, keepdims=True)
        prob_low = (exp_scores / row_total).astype(jnp.bfloat16)
        log_blocks.append((row_top + jnp.log(row_total))[..., 0])
        block_out = jnp.einsum("hqk,khd->qhd", prob_low, values, preferred_element_type=jnp.float32)
        out_blocks.append(block_out.astype(jnp.bfloat16))
    attn_heads = jnp.concatenate(out_blocks, axis=0)
    log_total = jnp.concatenate(log_blocks, axis=1)
    returned = lax.all_to_all(
        attn_heads.reshape(seq_len, 1, head_cols), "seq", split_axis=0, concat_axis=1, tiled=True
    )
    attended = returned.reshape(tok_rows, D)
    middle = acts + jnp.dot(attended, w_dense, preferred_element_type=jnp.float32) + bias_dense
    w_up = mlp_full[:, :FF]
    w_down_t = mlp_full[:, FF : 2 * FF]
    mlp_vectors = mlp_full[:, 2 * FF :].astype(jnp.float32)
    gain_two = mlp_vectors[:, 0]
    shift_two = mlp_vectors[:, 1]
    bias_up = mlp_vectors[:, 2 : 2 + UPC].T.reshape(FF)
    bias_down = mlp_vectors[:, 2 + UPC]
    normed_two, norm_two_back = jax.vjp(layer_norm, middle, gain_two, shift_two)
    normed_two_low = normed_two.astype(jnp.bfloat16)
    upper = jnp.dot(normed_two_low, w_up, preferred_element_type=jnp.float32) + bias_up
    active, gelu_back = jax.vjp(gelu_tanh, upper)
    active_low = active.astype(jnp.bfloat16)
    result = middle + contract_cols(active_low, w_down_t) + bias_down
    valid_float = valid_flags[0].astype(jnp.float32)
    cot_float = cotangent[0].astype(jnp.float32)
    deviation = result - teacher[0].astype(jnp.float32)
    valid_count, squared_sum = lax.psum(
        (jnp.sum(valid_float), jnp.sum(valid_float[:, None] * deviation * deviation)),
        ("seq", "wsh"),
    )
    distill = squared_sum / (valid_count * D)
    losses = jnp.stack([distill])
    result_grad = cot_float + valid_float[:, None] * (token_total / valid_count) * deviation
    down_grad = result_grad.astype(jnp.bfloat16)
    active_grad = jnp.dot(down_grad, w_down_t, preferred_element_type=jnp.float32)
    (upper_grad,) = gelu_back(active_grad)
    upper_low = upper_grad.astype(jnp.bfloat16)
    normed_two_grad = contract_cols(upper_low, w_up)
    middle_part, gain_two_grad, shift_two_grad = norm_two_back(normed_two_grad)
    middle_grad = result_grad + middle_part
    bias_up_grad = jnp.sum(upper_low, axis=0, dtype=jnp.float32)
    bias_down_grad = jnp.sum(down_grad, axis=0, dtype=jnp.float32)
    mlp_vec_grad = jnp.concatenate(
        [
            gain_two_grad[:, None],
            shift_two_grad[:, None],
            bias_up_grad.reshape(UPC, D).T,
            bias_down_grad[:, None],
        ],
        axis=1,
    )
    up_part = contract_rows(normed_two_low, upper_low)
    down_part = contract_rows(down_grad, active_low)
    vec_part = mlp_vec_grad
    mlp_gradient = lax.psum_scatter(
        jnp.concatenate([up_part, down_part, vec_part], axis=1),
        ("seq", "wsh"),
        scatter_dimension=0,
        tiled=True,
    )
    dense_grad = middle_grad.astype(jnp.bfloat16)
    attended_grad = contract_cols(dense_grad, w_dense).astype(jnp.bfloat16)
    grad_heads = lax.all_to_all(
        attended_grad.reshape(tok_rows, seq_size, head_cols),
        "seq",
        split_axis=1,
        concat_axis=0,
        tiled=True,
    )
    out_grad = grad_heads.reshape(seq_len, heads_here, DH)
    key_grad = jnp.zeros((seq_len, heads_here, DH), jnp.float32)
    value_grad = jnp.zeros((seq_len, heads_here, DH), jnp.float32)
    query_blocks = []
    for block_index in range(nblocks):
        row_start = block_index * QBLK
        key_end = seq_len
        q_rows = queries[row_start : row_start + QBLK]
        grad_rows = out_grad[row_start : row_start + QBLK]
        scores = block_scores(q_rows, keys_all, row_start, slopes, doc_row, score_scale)
        prob = jnp.exp(scores - log_total[:, row_start : row_start + QBLK, None])
        prob_low = prob.astype(jnp.bfloat16)
        prob_grad = jnp.einsum(
            "qhd,khd->hqk", grad_rows, values, preferred_element_type=jnp.float32
        )
        row_delta = jnp.sum(prob * prob_grad, axis=-1, keepdims=True)
        score_grad = (prob * (prob_grad - row_delta)).astype(jnp.bfloat16)
        query_blocks.append(
            jnp.einsum("hqk,khd->qhd", score_grad, keys_all, preferred_element_type=jnp.float32)
            * score_scale
        )
        key_grad = key_grad.at[:key_end].add(
            jnp.einsum("hqk,qhd->khd", score_grad, q_rows, preferred_element_type=jnp.float32)
            * score_scale
        )
        value_grad = value_grad.at[:key_end].add(
            jnp.einsum("hqk,qhd->khd", prob_low, grad_rows, preferred_element_type=jnp.float32)
        )
    query_grad = jnp.concatenate(query_blocks, axis=0)
    heads_grad = jnp.stack([query_grad, key_grad, value_grad], axis=1).astype(jnp.bfloat16)
    back_tokens = lax.all_to_all(
        heads_grad.reshape(seq_len, 3, 1, head_cols), "seq", split_axis=0, concat_axis=2, tiled=True
    )
    projected_grad = back_tokens.reshape(tok_rows, 3 * D)
    normed_grad = contract_cols(projected_grad, w_qkv)
    input_part, gain_one_grad, shift_one_grad = norm_one_back(normed_grad)
    input_grad = middle_grad + input_part
    qkv_sums = jnp.sum(projected_grad, axis=0, dtype=jnp.float32)
    bias_dense_grad = jnp.sum(dense_grad, axis=0, dtype=jnp.float32)
    attn_vec_grad = jnp.stack(
        [gain_one_grad, shift_one_grad, qkv_sums[:D], qkv_sums[2 * D :], bias_dense_grad], axis=1
    )
    qkv_part = contract_rows(normed_low, projected_grad)
    dense_part = contract_rows(attended, dense_grad)
    vec_part = attn_vec_grad
    attn_gradient = lax.psum_scatter(
        jnp.concatenate([qkv_part, dense_part, vec_part], axis=1),
        ("seq", "wsh"),
        scatter_dimension=0,
        tiled=True,
    )
    vector_gradient = jnp.concatenate(
        [attn_gradient[:, 4 * D :], mlp_gradient[:, 2 * FF :]], axis=1
    )
    attn_new, attn_first_new, attn_second_new = adam_update(
        attn_params, attn_first, attn_second, attn_gradient, step_count
    )
    mlp_new, mlp_first_new, mlp_second_new = adam_update(
        mlp_params, mlp_first, mlp_second, mlp_gradient, step_count
    )
    return (
        result.astype(jnp.bfloat16)[None],
        losses,
        input_grad[None],
        vector_gradient,
        attn_new,
        attn_first_new,
        attn_second_new,
        mlp_new,
        mlp_first_new,
        mlp_second_new,
    )


def solution(mesh):
    return jax.shard_map(
        shards,
        mesh=mesh,
        in_specs=(
            P("wsh", "seq", None),
            P("wsh", "seq", None),
            P("wsh", "seq", None),
            P("wsh", None),
            P("wsh", "seq"),
            P(),
            P(("seq", "wsh"), None),
            P(("seq", "wsh"), None),
            P(("seq", "wsh"), None),
            P(("seq", "wsh"), None),
            P(("seq", "wsh"), None),
            P(("seq", "wsh"), None),
        ),
        out_specs=(
            P("wsh", "seq", None),
            P(),
            P("wsh", "seq", None),
            P(("seq", "wsh"), None),
            P(("seq", "wsh"), None),
            P(("seq", "wsh"), None),
            P(("seq", "wsh"), None),
            P(("seq", "wsh"), None),
            P(("seq", "wsh"), None),
            P(("seq", "wsh"), None),
        ),
        check_vma=False,
    )
```

profile of v0, /device:TPU:0, one launch (start us, length us, event | category | flops | bytes accessed | tf_op | source)
XLA Modules:
  0.0 3008.5 jit_solution(13557915332097437351)
XLA Ops:
  15.1 195.8 %all-gather.3.cloned.1.call-done = bf16[2048,8197]{1,0:T(8,128)(2,1)} async-done(((bf16[64,8197]{1,0:T(8,128)(2,1)}), bf16[2048,8197]{1,0:T(8,128)(2,1)}) %all-gather.3.cloned.1.call-update) | async-done | bytes 33574928 | tf_op jit(solution)/shard_map/all_gather | solution.py:99
  215.2 15.3 fusion.24
  230.5 7.4 reshape.558
  252.5 134.6 %all-to-all-done = bf16[256,3,4,512]{3,0,1,2:T(8,128)(2,1)} async-done(((bf16[256,3,4,512]{3,0,1,2:T(8,128)(2,1)}), bf16[256,3,4,512]{3,0,1,2:T(8,128)(2,1)}, u32[]{:S(2)}, u32[]{:S(2)}) %all-to-all-start) | async-done | bytes 3145760 | tf_op jit(solution)/shard_map/all_to_all | solution.py:118
  430.4 59.6 %all-to-all-done.1 = bf16[4,2,65536]{2,1,0:T(2,128)(2,1)} async-done(((bf16[4,2,65536]{2,1,0:T(2,128)(2,1)}), bf16[4,2,65536]{2,1,0:T(2,128)(2,1)}, u32[]{:S(2)}, u32[]{:S(2)}) %all-to-all-start.1) | async-done | bytes 1048608 | tf_op jit(solution)/shard_map/all_to_all | solution.py:144
  502.8 140.8 %all-gather.5.cloned.1.call-done = bf16[2048,16391]{1,0:T(8,128)(2,1)} async-done(((bf16[64,16391]{1,0:T(8,128)(2,1)}), bf16[2048,16391]{1,0:T(8,128)(2,1)}) %all-gather.5.cloned.1.call-update) | async-done | bytes 67137552 | tf_op jit(solution)/shard_map/all_gather | solution.py:100
  646.9 17.3 fusion.12
  664.2 19.4 fusion.78
  683.6 37.9 %all-reduce = (f32[]{:T(128)}, f32[]{:T(128)}) all-reduce(f32[]{:T(128)} %get-tuple-element.168, f32[]{:T(128)} %convert_reduce_fusion.5), channel_id=1, replica_groups=mesh['seq'=4,'wsh'=8] {'seq','wsh'}, use_global_device_ids=true, to_apply=%region_9.10 | all-reduce | flops 2 | bytes 16 | tf_op jit(solution)/shard_map/psum | solution.py:165
  726.8 22.8 convert_reduce_fusion
  749.6 16.3 multiply_reduce_fusion.2
  779.2 25.1 all-to-all-done.2
  862.1 9.6 pad_maximum_fusion
  878.1 8.1 fusion.130
  886.2 83.3 %all-to-all-done.3 = bf16[1024,3,1,512]{3,1,2,0:T(4,128)(2,1)} async-done(((bf16[1024,3,1,512]{3,1,2,0:T(4,128)(2,1)}), bf16[1024,3,1,512]{3,1,2,0:T(4,128)(2,1)}, u32[]{:S(2)}, u32[]{:S(2)}) %all-to-all-start.3) | async-done | bytes 3145760 | tf_op jit(solution)/shard_map/all_to_all | solution.py:238
  979.3 21.5 fusion.92
  1000.8 12.8 fusion.118
  1020.6 77.6 %concatenate.38 = f32[2048,8197]{1,0:T(8,128)} concatenate(f32[2048,6144]{1,0:T(8,128)} %fusion.92, f32[2048,2048]{1,0:T(8,128)} %fusion.130, f32[2048,1]{1,0:T(8,128)} %copy.120, f32[2048,1]{1,0:T(8,128)} %copy.121, f32[2048,1]{1,0:T(8,128)} %bitcast.184, f32[2048,1]{1,0:T(8,128)} %bitcast.185, f32[2048,1]{1,0:T(8,128)S(1)} %copy-done.20), dimensions={1} | concatenate | bytes 134299648 | tf_op jit(solution)/shard_map/concatenate | solution.py:254
  1103.4 28.2 fusion.117
  1131.6 27.5 fusion.113
  1159.1 174.6 %concatenate.39 = f32[2048,16391]{1,0:T(8,128)} concatenate(f32[2048,8192]{1,0:T(8,128)} %fusion.117, f32[2048,8192]{1,0:T(8,128)} %fusion.113, f32[2048,1]{1,0:T(8,128)} %copy.126, f32[2048,1]{1,0:T(8,128)} %copy.127, f32[2048,4]{1,0:T(8,128)} %bitcast.183, f32[2048,1]{1,0:T(8,128)S(1)} %copy.128), dimensions={1} | concatenate | bytes 268550144 | tf_op jit(solution)/shard_map/concatenate | solution.py:194
  1340.4 470.5 %reduce-scatter.3.cloned.1.call-done = f32[64,8197]{1,0:T(8,128)} async-done(((f32[2048,8197]{1,0:T(8,128)}), f32[64,8197]{1,0:T(8,128)}) %reduce-scatter.3.cloned.1.call-update) | async-done | bytes 2098448 | tf_op jit(solution)/shard_map/reduce_scatter | solution.py:253
  1818.9 1168.7 %reduce-scatter.5.cloned.1.call-done = f32[64,16391]{1,0:T(8,128)} async-done(((f32[2048,16391]{1,0:T(8,128)}), f32[64,16391]{1,0:T(8,128)}) %reduce-scatter.5.cloned.1.call-update) | async-done | bytes 4196112 | tf_op jit(solution)/shard_map/reduce_scatter | solution.py:193
  2989.0 11.6 multiply_subtract_fusion
  (245 shorter events, 203.5 us)
Async XLA Ops:
  7.2 203.7 %all-gather.3.cloned.1.call-start = ((), (), s32[]{:S(2)}) async-start(), calls=%async_computation.6 | async-start | bytes 35143680 | tf_op jit(solution)/shard_map/all_gather | solution.py:99
  9.9 633.7 %all-gather.5.cloned.1.call-start = ((), (), s32[]{:S(2)}) async-start(), calls=%async_computation.7 | async-start | bytes 69746688 | tf_op jit(solution)/shard_map/all_gather | solution.py:100
  14.1 216.4 %copy-start.44 = (f32[256]{0:T(256)}, f32[256]{0:T(256)S(1)}, u32[]{:S(2)}) copy-start(f32[256]{0:T(256)S(1)} %broadcast_multiply_fusion.2) | copy-start | bytes 3076
  15.1 215.4 %copy-start.47 = (f32[256]{0:T(256)}, f32[256]{0:T(256)S(1)}, u32[]{:S(2)}) copy-start(f32[256]{0:T(256)S(1)} %fusion.111) | copy-start | bytes 3076
  242.1 145.0 %all-to-all-start = ((bf16[256,3,4,512]{3,0,1,2:T(8,128)(2,1)}), bf16[256,3,4,512]{3,0,1,2:T(8,128)(2,1)}, u32[]{:S(2)}, u32[]{:S(2)}) async-start(bf16[256,3,4,512]{3,0,1,2:T(8,128)(2,1)} %copy.94), calls=%async_computation | async-start | bytes 6291456 | tf_op jit(solution)/shard_map/all_to_all | solution.py:118
  399.6 10.3 copy-start.10
  401.6 16.8 copy-start.12
  425.6 64.5 %all-to-all-start.1 = ((bf16[4,2,65536]{2,1,0:T(2,128)(2,1)}), bf16[4,2,65536]{2,1,0:T(2,128)(2,1)}, u32[]{:S(2)}, u32[]{:S(2)}) async-start(bf16[4,2,65536]{2,1,0:T(2,128)(2,1)} %reshape.575), calls=%async_computation.1 | async-start | bytes 2097152 | tf_op jit(solution)/shard_map/all_to_all | solution.py:144
  502.4 263.5 %copy-start.8 = (f32[256,2048]{1,0:T(8,128)}, f32[256,2048]{1,0:T(8,128)S(1)}, u32[]{:S(2)}) copy-start(f32[256,2048]{1,0:T(8,128)S(1)} %get-tuple-element.167) | copy-start | bytes 6291460
  502.4 263.5 %copy-start.40 = (f32[256]{0:T(256)}, f32[256]{0:T(256)S(1)}, u32[]{:S(2)}) copy-start(f32[256]{0:T(256)S(1)} %broadcast_multiply_fusion.1) | copy-start | bytes 3076
  502.8 263.1 %copy-start.42 = (f32[256]{0:T(256)}, f32[256]{0:T(256)S(1)}, u32[]{:S(2)}) copy-start(f32[256]{0:T(256)S(1)} %fusion.112) | copy-start | bytes 3076
  646.2 18.0 copy-start.36
  646.2 119.7 %copy-start.30 = (f32[2048]{0:T(1024)}, f32[2048]{0:T(1024)S(1)}, u32[]{:S(2)}) copy-start(f32[2048]{0:T(1024)S(1)} %get-tuple-element.127) | copy-start | bytes 24580
  646.9 17.3 copy-start.29
  726.8 39.7 %copy-start.2 = (f32[256,2048]{1,0:T(8,128)}, f32[256,2048]{1,0:T(8,128)S(1)}, u32[]{:S(2)}) copy-start(f32[256,2048]{1,0:T(8,128)S(1)} %get-tuple-element.146) | copy-start | bytes 6291460
  773.5 32.2 %copy-start.13 = (bf16[1024,1,4,128]{0,3,2,1:T(8,128)(2,1)S(1)}, bf16[1024,1,4,128]{0,3,2,1:T(8,128)(2,1)}, u32[]{:S(2)}) copy-start(bf16[1024,1,4,128]{0,3,2,1:T(8,128)(2,1)} %copy-done.12) | copy-start | bytes 3145732
  774.5 29.8 all-to-all-start.2
  822.3 12.0 slice-start
  871.7 97.7 %all-to-all-start.3 = ((bf16[1024,3,1,512]{3,1,2,0:T(4,128)(2,1)}), bf16[1024,3,1,512]{3,1,2,0:T(4,128)(2,1)}, u32[]{:S(2)}, u32[]{:S(2)}) async-start(bf16[1024,3,1,512]{3,1,2,0:T(4,128)(2,1)} %pad_maximum_fusion), calls=%async_computation.3 | async-start | bytes 8388608 | tf_op jit(solution)/shard_map/all_to_all | solution.py:238
  876.7 934.1 %reduce-scatter.3.cloned.1.call-start = ((), (), s32[]{:S(2)}) async-start(), calls=%async_computation.8 | async-start | bytes 70287360 | tf_op jit(solution)/shard_map/reduce_scatter | solution.py:253
  1000.8 12.9 copy-start.54
  1013.7 84.6 %copy-start.16 = (f32[256,2048]{1,0:T(8,128)}, f32[256,2048]{1,0:T(8,128)S(1)}, u32[]{:S(2)}) copy-start(f32[256,2048]{1,0:T(8,128)S(1)} %get-tuple-element.175) | copy-start | bytes 6291460
  1098.4 1889.2 %reduce-scatter.5.cloned.1.call-start = ((), (), s32[]{:S(2)}) async-start(), calls=%async_computation.9 | async-start | bytes 139493376 | tf_op jit(solution)/shard_map/reduce_scatter | solution.py:193
  1103.4 28.2 copy-start.3
  (49 other events, 208.6 us)
Sparse Core Ops, SparseCore 0:
  11.4 199.4 all-gather.2
  214.4 429.1 all-gather.4
  1098.5 712.3 reduce-scatter.2
  1817.1 1170.3 reduce-scatter.4
where the time goes:
time: 3020 us; the launch traced here: 3010 us
  waiting for transfers between devices  2280 us (75%)
  local copies, waits for them, and re-layouts  340 us (11%)
  matrix products  239 us (8%)
  other arithmetic  74.3 us (2%)
  blocking collectives  37.9 us (1%)
    reduce_scatter x1, waiting for transfers between devices, shards(): lax.psum_scatter(jnp.concatenate([up_part, down_part, vec_part], axis=1),...  1170 us
    reduce_scatter x1, waiting for transfers between devices, shards(): lax.psum_scatter(jnp.concatenate([qkv_part, dense_part, vec_part], axis=1...  470 us
    all_gather x1, waiting for transfers between devices, shards(): lax.all_gather(attn_low, ('seq', 'wsh'), axis=0, tiled=True)  196 us
    concatenate x1, local copies, waits for them, and re-layouts, shards(): jnp.concatenate([up_part, down_part, vec_part], axis=1)  175 us
    all_gather x1, waiting for transfers between devices, shards(): lax.all_gather(mlp_low, ('seq', 'wsh'), axis=0, tiled=True)  141 us
    all_to_all x1, waiting for transfers between devices, shards(): lax.all_to_all(sent, 'seq', split_axis=2, concat_axis=0, tiled=True)  135 us
    dot_general x4, matrix products, contract_rows(): lax.dot_general(left, right, (((0,), (0,)), ((), ())), preferred_element_...  85.3 us
    all_to_all x1, waiting for transfers between devices, shards(): lax.all_to_all(heads_grad.reshape(seq_len, 3, 1, head_cols), 'seq', split...  83.3 us
  transfers between devices with their start and end apart: 8, of which 8 were waited for; matrix products, arithmetic and copies ran while one was open for 12% of the time, Pallas kernels for 0%

commit v1 on v0

v1 whole, which is shorter than its diff:
```python
import math

import jax
import jax.numpy as jnp
from jax import lax
from jax.sharding import PartitionSpec as P

D = 2048
H = 16
DH = 128
FF = 8192
QBLK = 512
UPC = 4

eps_norm = 1e-05
beta_one = 0.9
beta_two = 0.95
adam_eps = 1e-08
decay_rate = 0.1
learn_rate = 0.05
gelu_coef = 0.7978845608028654
BF = jnp.bfloat16
F32 = jnp.float32


def norm_stats(value):
    row_mean = jnp.mean(value, axis=-1, keepdims=True)
    centred = value - row_mean
    variance = jnp.mean(centred * centred, axis=-1, keepdims=True)
    scale = lax.rsqrt(variance + eps_norm)
    return centred * scale, scale


def norm_back(grad, gain, hat, scale):
    e = grad * gain
    return scale * (
        e
        - jnp.mean(e, axis=-1, keepdims=True)
        - hat * jnp.mean(e * hat, axis=-1, keepdims=True)
    )


def gelu_tanh(value):
    return 0.5 * value * (1.0 + jnp.tanh(gelu_coef * (value + 0.044715 * value * value * value)))


def adam_update(weights, first, second, gradient, step_count):
    steps_done = step_count[0].astype(F32)
    first_new = beta_one * first + (1.0 - beta_one) * gradient
    second_new = beta_two * second + (1.0 - beta_two) * gradient * gradient
    fix_one = 1.0 - jnp.power(beta_one, steps_done)
    fix_two = 1.0 - jnp.power(beta_two, steps_done)
    update = first_new / fix_one / (jnp.sqrt(second_new / fix_two) + adam_eps)
    return (weights - learn_rate * (update + decay_rate * weights), first_new, second_new)


def contract_rows(left, right, out=F32):
    return lax.dot_general(
        left, right, (((0,), (0,)), ((), ())), preferred_element_type=F32
    ).astype(out)


def contract_cols(left, right, out=F32):
    return lax.dot_general(
        left, right, (((1,), (1,)), ((), ())), preferred_element_type=F32
    ).astype(out)


def dot(left, right):
    return jnp.dot(left, right, preferred_element_type=F32)


def block_scores(q_rows, key_rows, row_start, slopes, doc_row, score_scale):
    rows_here = q_rows.shape[0]
    keys_here = key_rows.shape[0]
    scores = (
        jnp.einsum("qhd,khd->hqk", q_rows, key_rows, preferred_element_type=F32) * score_scale
    )
    row_pos = row_start + jnp.arange(rows_here, dtype=jnp.int32)
    key_pos = jnp.arange(keys_here, dtype=jnp.int32)
    distance = (row_pos[:, None] - key_pos[None, :]).astype(F32)
    scores = scores - slopes[:, None, None] * distance[None]
    doc_rows = doc_row[row_start : row_start + rows_here]
    allowed = (doc_rows[:, None] == doc_row[None, :]) & (key_pos[None, :] <= row_pos[:, None])
    return jnp.where(allowed[None], scores, -jnp.inf)


def shards(
    inputs,
    cotangent,
    teacher,
    document_ids,
    valid_flags,
    step_count,
    attn_params,
    attn_first,
    attn_second,
    mlp_params,
    mlp_first,
    mlp_second,
):
    tok_rows = inputs.shape[1]
    seq_size = lax.axis_size("seq")
    wsh_size = lax.axis_size("wsh")
    seq_at = lax.axis_index("seq")
    wsh_at = lax.axis_index("wsh")
    own_rows = attn_params.shape[0]
    seq_len = tok_rows * seq_size
    token_total = seq_len * wsh_size
    heads_here = H // seq_size
    head_cols = heads_here * DH
    ff_cols = FF // wsh_size
    score_scale = 1.0 / math.sqrt(DH)
    nblocks = seq_len // QBLK

    own_vectors = jnp.concatenate([attn_params[:, 4 * D :], mlp_params[:, 2 * FF :]], axis=1)
    vectors = lax.all_gather(own_vectors.astype(BF), ("seq", "wsh"), axis=0, tiled=True).astype(F32)
    gain_one, shift_one, bias_query, bias_value, bias_dense = (vectors[:, i] for i in range(5))
    gain_two, shift_two = vectors[:, 5], vectors[:, 6]
    bias_up = vectors[:, 7 : 7 + UPC].T.reshape(FF)
    bias_down = vectors[:, 7 + UPC]

    inputs_all = lax.all_gather(inputs[0], "seq", axis=0, tiled=True)

    qkv_own = attn_params[:, : 3 * D].astype(BF).reshape(own_rows, 3, seq_size, head_cols)
    qkv_cols = lax.all_to_all(
        qkv_own.transpose(2, 0, 1, 3), "seq", split_axis=0, concat_axis=0, tiled=True
    )
    w_qkv = lax.all_gather(qkv_cols, "wsh", axis=1)
    w_qkv = w_qkv.reshape(D, 3 * head_cols)
    w_dense = lax.all_gather(attn_params[:, 3 * D : 4 * D].astype(BF), "wsh", axis=0, tiled=True)

    mlp_own = mlp_params[:, : 2 * FF].astype(BF).reshape(own_rows, 2, wsh_size, ff_cols)
    mlp_cols = lax.all_to_all(
        mlp_own.transpose(2, 0, 1, 3), "wsh", split_axis=0, concat_axis=0, tiled=True
    )
    w_mlp = lax.all_gather(
        mlp_cols.reshape(wsh_size * own_rows, 2 * ff_cols), "seq", axis=0, tiled=True
    )
    w_up = w_mlp[:, :ff_cols]
    w_down_t = w_mlp[:, ff_cols:]

    valid_float = valid_flags[0].astype(F32)
    valid_count = lax.psum(jnp.sum(valid_float), ("seq", "wsh"))

    normed_low = (norm_stats(inputs_all.astype(F32))[0] * gain_one + shift_one).astype(BF)
    acts = inputs[0].astype(F32)
    hat_one, scale_one = norm_stats(acts)
    bias_q = lax.dynamic_slice(bias_query, (seq_at * head_cols,), (head_cols,))
    bias_v = lax.dynamic_slice(bias_value, (seq_at * head_cols,), (head_cols,))
    qkv_bias = jnp.concatenate([bias_q, jnp.zeros_like(bias_q), bias_v])
    projected = (dot(normed_low, w_qkv) + qkv_bias).astype(BF)
    arrived = projected.reshape(seq_len, 3, heads_here, DH)
    queries = arrived[:, 0]
    keys_all = arrived[:, 1]
    values = arrived[:, 2]
    head_ids = seq_at * heads_here + jnp.arange(heads_here, dtype=jnp.int32)
    slopes = jnp.exp2(-8.0 * (head_ids.astype(F32) + 1.0) / H)
    doc_row = document_ids[0]
    out_blocks = []
    log_blocks = []
    for block_index in range(nblocks):
        row_start = block_index * QBLK
        scores = block_scores(
            queries[row_start : row_start + QBLK], keys_all, row_start, slopes, doc_row, score_scale
        )
        row_top = jnp.max(scores, axis=-1, keepdims=True)
        exp_scores = jnp.exp(scores - row_top)
        row_total = jnp.sum(exp_scores, axis=-1, keepdims=True)
        prob_low = (exp_scores / row_total).astype(BF)
        log_blocks.append((row_top + jnp.log(row_total))[..., 0])
        block_out = jnp.einsum("hqk,khd->qhd", prob_low, values, preferred_element_type=F32)
        out_blocks.append(block_out.astype(BF))
    attended = jnp.concatenate(out_blocks, axis=0).reshape(seq_len, head_cols)
    log_total = jnp.concatenate(log_blocks, axis=1)
    dense_out = lax.psum_scatter(
        dot(attended, w_dense).astype(BF), "seq", scatter_dimension=0, tiled=True
    )
    middle = acts + dense_out.astype(F32) + bias_dense

    hat_two, scale_two = norm_stats(middle)
    normed_two_low = (hat_two * gain_two + shift_two).astype(BF)
    normed_two_all = lax.all_gather(normed_two_low, "wsh", axis=0, tiled=True)
    bias_up_here = lax.dynamic_slice(bias_up, (wsh_at * ff_cols,), (ff_cols,))
    upper = dot(normed_two_all, w_up) + bias_up_here
    active, gelu_back = jax.vjp(gelu_tanh, upper)
    active_low = active.astype(BF)
    down_out = lax.psum_scatter(
        contract_cols(active_low, w_down_t, BF), "wsh", scatter_dimension=0, tiled=True
    )
    result = middle + down_out.astype(F32) + bias_down

    cot_float = cotangent[0].astype(F32)
    deviation = result - teacher[0].astype(F32)
    squared_sum = lax.psum(jnp.sum(valid_float[:, None] * deviation * deviation), ("seq", "wsh"))
    losses = jnp.stack([squared_sum / (valid_count * D)])
    result_grad = cot_float + valid_float[:, None] * (token_total / valid_count) * deviation
    down_grad = result_grad.astype(BF)

    down_grad_all = lax.all_gather(down_grad, "wsh", axis=0, tiled=True)
    (upper_grad,) = gelu_back(dot(down_grad_all, w_down_t))
    upper_low = upper_grad.astype(BF)
    normed_two_grad = lax.psum_scatter(
        contract_cols(upper_low, w_up, BF), "wsh", scatter_dimension=0, tiled=True
    ).astype(F32)
    up_part = contract_rows(normed_two_all, upper_low, BF)
    down_part = contract_rows(down_grad_all, active_low, BF)
    mlp_rows = lax.psum_scatter(
        jnp.concatenate([up_part, down_part], axis=1), "seq", scatter_dimension=0, tiled=True
    )
    mlp_gradient = lax.all_to_all(
        mlp_rows.reshape(wsh_size, own_rows, 2, ff_cols),
        "wsh",
        split_axis=0,
        concat_axis=0,
        tiled=True,
    )
    mlp_gradient = mlp_gradient.transpose(1, 2, 0, 3).reshape(own_rows, 2 * FF).astype(F32)
    middle_grad = result_grad + norm_back(normed_two_grad, gain_two, hat_two, scale_two)

    dense_grad = middle_grad.astype(BF)
    dense_grad_all = lax.all_gather(dense_grad, "seq", axis=0, tiled=True)
    out_grad = contract_cols(dense_grad_all, w_dense, BF).reshape(seq_len, heads_here, DH)
    dense_part = contract_rows(attended, dense_grad_all, BF)
    key_grad = jnp.zeros((seq_len, heads_here, DH), F32)
    value_grad = jnp.zeros((seq_len, heads_here, DH), F32)
    query_blocks = []
    for block_index in range(nblocks):
        row_start = block_index * QBLK
        q_rows = queries[row_start : row_start + QBLK]
        grad_rows = out_grad[row_start : row_start + QBLK]
        scores = block_scores(q_rows, keys_all, row_start, slopes, doc_row, score_scale)
        prob = jnp.exp(scores - log_total[:, row_start : row_start + QBLK, None])
        prob_low = prob.astype(BF)
        prob_grad = jnp.einsum("qhd,khd->hqk", grad_rows, values, preferred_element_type=F32)
        row_delta = jnp.sum(prob * prob_grad, axis=-1, keepdims=True)
        score_grad = (prob * (prob_grad - row_delta)).astype(BF)
        query_blocks.append(
            jnp.einsum("hqk,khd->qhd", score_grad, keys_all, preferred_element_type=F32)
            * score_scale
        )
        key_grad = key_grad + (
            jnp.einsum("hqk,qhd->khd", score_grad, q_rows, preferred_element_type=F32)
            * score_scale
        )
        value_grad = value_grad + jnp.einsum(
            "hqk,qhd->khd", prob_low, grad_rows, preferred_element_type=F32
        )
    query_grad = jnp.concatenate(query_blocks, axis=0)
    projected_grad = (
        jnp.stack([query_grad, key_grad, value_grad], axis=1)
        .astype(BF)
        .reshape(seq_len, 3 * head_cols)
    )
    normed_grad = lax.psum_scatter(
        contract_cols(projected_grad, w_qkv, BF), "seq", scatter_dimension=0, tiled=True
    ).astype(F32)
    input_grad = middle_grad + norm_back(normed_grad, gain_one, hat_one, scale_one)
    qkv_part = contract_rows(normed_low, projected_grad, BF)
    qkv_rows = lax.psum_scatter(
        qkv_part.reshape(seq_size, wsh_size, own_rows, 3 * head_cols),
        "wsh",
        scatter_dimension=1,
        tiled=True,
    ).reshape(seq_size, own_rows, 3, head_cols)
    qkv_gradient = lax.all_to_all(qkv_rows, "seq", split_axis=0, concat_axis=0, tiled=True)
    qkv_gradient = qkv_gradient.transpose(1, 2, 0, 3).reshape(own_rows, 3 * D)
    dense_gradient = lax.psum_scatter(dense_part, "wsh", scatter_dimension=0, tiled=True)
    attn_gradient = jnp.concatenate([qkv_gradient, dense_gradient], axis=1).astype(F32)

    zeros = jnp.zeros((D,), F32)
    qkv_sums = jnp.sum(projected_grad, axis=0, dtype=F32)
    query_sums = lax.dynamic_update_slice(zeros, qkv_sums[:head_cols], (seq_at * head_cols,))
    value_sums = lax.dynamic_update_slice(zeros, qkv_sums[2 * head_cols :], (seq_at * head_cols,))
    up_sums = lax.dynamic_update_slice(
        jnp.zeros((FF,), F32), jnp.sum(upper_low, axis=0, dtype=F32), (wsh_at * ff_cols,)
    )
    vector_part = jnp.concatenate(
        [
            jnp.stack(
                [
                    jnp.sum(normed_grad * hat_one, axis=0),
                    jnp.sum(normed_grad, axis=0),
                    query_sums,
                    value_sums,
                    jnp.sum(dense_grad, axis=0, dtype=F32),
                    jnp.sum(normed_two_grad * hat_two, axis=0),
                    jnp.sum(normed_two_grad, axis=0),
                ],
                axis=1,
            ),
            up_sums.reshape(UPC, D).T,
            jnp.sum(down_grad, axis=0, dtype=F32)[:, None],
        ],
        axis=1,
    )
    vector_gradient = lax.psum_scatter(
        vector_part, ("seq", "wsh"), scatter_dimension=0, tiled=True
    )
    attn_gradient = jnp.concatenate([attn_gradient, vector_gradient[:, :5]], axis=1)
    mlp_gradient = jnp.concatenate([mlp_gradient, vector_gradient[:, 5:]], axis=1)
    attn_new, attn_first_new, attn_second_new = adam_update(
        attn_params, attn_first, attn_second, attn_gradient, step_count
    )
    mlp_new, mlp_first_new, mlp_second_new = adam_update(
        mlp_params, mlp_first, mlp_second, mlp_gradient, step_count
    )
    return (
        result.astype(BF)[None],
        losses,
        input_grad[None],
        vector_gradient,
        attn_new,
        attn_first_new,
        attn_second_new,
        mlp_new,
        mlp_first_new,
        mlp_second_new,
    )


def solution(mesh):
    rows = P(("seq", "wsh"), None)
    tokens = P("wsh", "seq", None)
    return jax.shard_map(
        shards,
        mesh=mesh,
        in_specs=(tokens, tokens, tokens, P("wsh", None), P("wsh", "seq"), P()) + (rows,) * 6,
        out_specs=(tokens, P(), tokens) + (rows,) * 7,
        check_vma=False,
    )
```

time: 3020 us -> 1390 us (0.46)
  waiting for transfers between devices: 2280 us -> 809 us
  local copies, waits for them, and re-layouts: 340 us -> 86.3 us
  blocking collectives: 37.9 us -> 220 us
  matrix products: 239 us -> 170 us
    reduce_scatter x2 -> x7, waiting for transfers between devices: 1640 us -> 372 us  [the longest x1 128 us: shards(): lax.psum_scatter(jnp.concatenate([up_part, down_part], axis=1), 'seq', sc...]
    all_to_all x4 -> x2, waiting for transfers between devices: 303 us -> 7.34 us  [the longest x1 7.33 us: shards(): lax.all_to_all(qkv_rows, 'seq', split_axis=0, concat_axis=0, tiled=True)]
    concatenate x2 -> x1, local copies, waits for them, and re-layouts: 252 us -> 0.27 us  [shards(): jnp.concatenate([jnp.stack([jnp.sum(normed_grad * hat_one, axis=0), jnp.s...]
    all_to_all x0 -> x2, blocking collectives: none -> 73.9 us  [the longest x1 44.8 us: shards(): lax.all_to_all(qkv_own.transpose(2, 0, 1, 3), 'seq', split_axis=0, concat...]
    psum x1 -> x2, blocking collectives: 37.9 us -> 101 us  [the longest x1 60.2 us: shards(): lax.psum(jnp.sum(valid_float[:, None] * deviation * deviation), ('seq', '...]
    unnamed x4 -> x16, waiting for transfers between devices: 0.07 us -> 54.6 us
    all_gather x0 -> x1, blocking collectives: none -> 45.4 us  [shards(): lax.all_gather(own_vectors.astype(BF), ('seq', 'wsh'), axis=0, tiled=True)]
    dot_general x4, matrix products: 85.3 us -> 46 us  [contract_rows(): lax.dot_general(left, right, (((0,), (0,)), ((), ())), preferred_element_...]
  transfers between devices with their start and end apart: 8 -> 17, of which waited for: 8 -> 14; matrix products, arithmetic and copies ran while one was open for 12% -> 14% of each run, Pallas kernels for 0% -> 0%
where the time goes in v1:
time: 1390 us
  waiting for transfers between devices  809 us (58%)
  blocking collectives  220 us (16%)
  matrix products  170 us (12%)
  local copies, waits for them, and re-layouts  86.3 us (6%)
  other arithmetic  74.2 us (5%)
  between operations  18.9 us (1%)
    all_gather x1, waiting for transfers between devices, shards(): lax.all_gather(mlp_cols.reshape(wsh_size * own_rows, 2 * ff_cols), 'seq',...  147 us
    reduce_scatter x1, waiting for transfers between devices, shards(): lax.psum_scatter(jnp.concatenate([up_part, down_part], axis=1), 'seq', sc...  128 us
    all_gather x1, waiting for transfers between devices, shards(): dense_grad_all = lax.all_gather(dense_grad, 'seq', axis=0, tiled=True)  80.3 us
    reduce_scatter x1, waiting for transfers between devices, shards(): lax.psum_scatter(contract_cols(upper_low, w_up, BF), 'wsh', scatter_dimen...  71.4 us
    psum x1, blocking collectives, shards(): lax.psum(jnp.sum(valid_float[:, None] * deviation * deviation), ('seq', '...  60.2 us
    reduce_scatter x1, waiting for transfers between devices, shards(): lax.psum_scatter(qkv_part.reshape(seq_size, wsh_size, own_rows, 3 * head_...  60.1 us
    all_gather x1, waiting for transfers between devices, shards(): normed_two_all = lax.all_gather(normed_two_low, 'wsh', axis=0, tiled=True)  54.8 us
    unnamed x16, waiting for transfers between devices  54.6 us
  transfers between devices with their start and end apart: 17, of which 14 were waited for; matrix products, arithmetic and copies ran while one was open for 14% of the time, Pallas kernels for 0%

profile of v1, /device:TPU:0, one launch (start us, length us, event | category | flops | bytes accessed | tf_op | source)
XLA Modules:
  0.0 1388.0 jit_solution(16799740649493826731)
XLA Ops:
  10.5 44.8 %all_to_all.20 = bf16[4,64,3,512]{3,1,2,0:T(8,128)(2,1)S(1)} all-to-all(bf16[4,64,3,512]{3,1,2,0:T(8,128)(2,1)S(1)} %copy.202), channel_id=1, replica_groups=mesh['seq'=4,'wsh'=8] {'seq'}, dimensions={0} | all-to-all | bytes 1572864 | tf_op jit(solution)/shard_map/all_to_all | solution.py:126
  60.2 45.4 %all-gather.2 = bf16[32,64,12]{1,2,0:T(8,128)(2,1)S(1)} all-gather(bf16[1,64,12]{1,2,0:T(8,128)(2,1)S(1)} %maximum_bitcast_fusion.1), channel_id=1, replica_groups=mesh['seq'=4,'wsh'=8] {'seq','wsh'}, dimensions={0}, use_global_device_ids=true | all-gather | bytes 50688 | tf_op jit(solution)/shard_map/all_gather | solution.py:117
  114.1 38.3 %all-gather.23.cloned.1.call-done = bf16[4,512,3,512]{3,0,2,1:T(4,128)(2,1)} async-done(((bf16[4,64,3,512]{3,0,2,1:T(4,128)(2,1)}), bf16[4,512,3,512]{3,0,2,1:T(4,128)(2,1)}) %all-gather.23.cloned.1.call-update) | async-done | bytes 6291472 | tf_op jit(solution)/shard_map/all_gather | solution.py:129
  152.4 13.5 copy.204
  230.4 29.1 %all_to_all.21 = bf16[8,64,2,1024]{3,2,1,0:T(2,128)(2,1)S(1)} all-to-all(bf16[8,64,2,1024]{3,2,1,0:T(2,128)(2,1)S(1)} %bitcast.241), channel_id=1, replica_groups=mesh['seq'=4,'wsh'=8] {'wsh'}, dimensions={0} | all-to-all | bytes 4194304 | tf_op jit(solution)/shard_map/all_to_all | solution.py:134
  261.7 34.3 %reduce-scatter.11.cloned.1.call-done = bf16[256,2048]{1,0:T(8,128)(2,1)} async-done(((bf16[1024,2048]{1,0:T(8,128)(2,1)}), bf16[256,2048]{1,0:T(8,128)(2,1)}) %reduce-scatter.11.cloned.1.call-update) | async-done | bytes 1048592 | tf_op jit(solution)/shard_map/reduce_scatter | solution.py:176
  301.3 146.8 %all-gather.15.cloned.1.call-done = bf16[2048,2048]{1,0:T(8,128)(2,1)} async-done(((bf16[512,2048]{1,0:T(8,128)(2,1)}), bf16[2048,2048]{1,0:T(8,128)(2,1)}) %all-gather.15.cloned.1.call-update) | async-done | bytes 8388624 | tf_op jit(solution)/shard_map/all_gather | solution.py:137
  448.2 54.8 %all-gather.13.cloned.1.call-done = bf16[2048,2048]{1,0:T(8,128)(2,1)} async-done(((bf16[256,2048]{1,0:T(8,128)(2,1)}), bf16[2048,2048]{1,0:T(8,128)(2,1)}) %all-gather.13.cloned.1.call-update) | async-done | bytes 8388624 | tf_op jit(solution)/shard_map/all_gather | solution.py:183
  503.0 14.5 %fusion.32 = f32[2048,1024]{1,0:T(8,128)} fusion(bf16[2048,2048]{1,0:T(8,128)(2,1)} %all-gather.13.cloned.1.call-done, bf16[2048,2048]{1,0:T(8,128)(2,1)} %all-gather.15.cloned.1.call-done), kind=kOutput, calls=%fused_computation.64 | convolution fusion | flops 8589934592 | bytes 20971520 | tf_op jit(solution)/shard_map/dot_general | solution.py:70
  517.5 17.0 %convolution_convert_fusion.2 = bf16[2048,2048]{1,0:T(8,128)(2,1)} fusion(bf16[2048,2048]{1,0:T(8,128)(2,1)S(1)} %copy-done.38, f32[2048,1024]{1,0:T(8,128)} %fusion.32, f32[1024]{0:T(1024)S(1)} %dynamic_slice.17), kind=kOutput, calls=%fused_computation.36 | convolution fusion | flops 8615100416 | bytes 20975616 | tf_op jit(solution)/shard_map/dot_general | solution.py:64
  535.7 40.3 %psum.15 = f32[]{:T(128)} all-reduce(f32[]{:T(128)} %convert_reduce_fusion.8), channel_id=1, replica_groups=mesh['seq'=4,'wsh'=8] {'seq','wsh'}, use_global_device_ids=true, to_apply=%region_13.14 | all-reduce | flops 1 | bytes 8 | tf_op jit(solution)/shard_map/psum | solution.py:144
  576.7 30.0 %reduce-scatter.13.cloned.1.call-done = bf16[256,2048]{1,0:T(8,128)(2,1)} async-done(((bf16[2048,2048]{1,0:T(8,128)(2,1)}), bf16[256,2048]{1,0:T(8,128)(2,1)}) %reduce-scatter.13.cloned.1.call-update) | async-done | bytes 1048592 | tf_op jit(solution)/shard_map/reduce_scatter | solution.py:188
  610.9 54.4 %all-gather.17.cloned.1.call-done = bf16[2048,2048]{1,0:T(8,128)(2,1)} async-done(((bf16[256,2048]{1,0:T(8,128)(2,1)}), bf16[2048,2048]{1,0:T(8,128)(2,1)}) %all-gather.17.cloned.1.call-update) | async-done | bytes 8388624 | tf_op jit(solution)/shard_map/all_gather | solution.py:200
  665.3 19.7 %convert_reduce_fusion.1 = (f32[1024]{0:T(1024)S(1)}, bf16[2048,1024]{1,0:T(8,128)(2,1)S(1)}) fusion(bf16[2048,2048]{1,0:T(8,128)(2,1)} %all-gather.17.cloned.1.call-done, bf16[2048,2048]{1,0:T(8,128)(2,1)} %all-gather.15.cloned.1.call-done, f32[2048,1024]{1,0:T(8,128)} %fusion.32, f32[1024]{0:T(1024)S(1)} %dynamic_slice.17), kind=kOutput, calls=%fused_computation.20 | convolution fusion | flops 8646556672 | bytes 25174016 | tf_op jit(solution)/shard_map/dot_general | solution.py:70
  687.0 13.1 convolution_convert_fusion.1
  700.4 71.4 %reduce-scatter.15.cloned.1.call-done = bf16[256,2048]{1,0:T(8,128)(2,1)} async-done(((bf16[2048,2048]{1,0:T(8,128)(2,1)}), bf16[256,2048]{1,0:T(8,128)(2,1)}) %reduce-scatter.15.cloned.1.call-update) | async-done | bytes 1048592 | tf_op jit(solution)/shard_map/reduce_scatter | solution.py:203
  780.3 80.3 %all-gather.19.cloned.1.call-done = bf16[1024,2048]{1,0:T(8,128)(2,1)} async-done(((bf16[256,2048]{1,0:T(8,128)(2,1)}), bf16[1024,2048]{1,0:T(8,128)(2,1)}) %all-gather.19.cloned.1.call-update) | async-done | bytes 4194320 | tf_op jit(solution)/shard_map/all_gather | solution.py:222
  903.9 13.9 %convolution_convert_fusion.6 = bf16[2048,1024]{0,1:T(8,128)(2,1)} fusion(bf16[2048,2048]{1,0:T(8,128)(2,1)} %all-gather.13.cloned.1.call-done, bf16[2048,1024]{1,0:T(8,128)(2,1)} %copy-done.40), kind=kOutput, calls=%fused_computation.59 | convolution fusion | flops 8592031744 | bytes 16777216 | tf_op jit(solution)/shard_map/dot_general | solution.py:58
  917.8 16.5 %convolution_convert_fusion.5 = bf16[2048,1024]{0,1:T(8,128)(2,1)} fusion(bf16[2048,2048]{1,0:T(8,128)(2,1)} %all-gather.17.cloned.1.call-done, f32[2048,1024]{1,0:T(8,128)} %fusion.32, f32[1024]{0:T(1024)S(1)} %dynamic_slice.17), kind=kOutput, calls=%fused_computation.58 | convolution fusion | flops 8613003264 | bytes 20975616 | tf_op jit(solution)/shard_map/dot_general | solution.py:58
  943.4 35.8 %reduce-scatter.17.cloned.1.call-done = bf16[256,2048]{1,0:T(8,128)(2,1)} async-done(((bf16[1024,2048]{1,0:T(8,128)(2,1)}), bf16[256,2048]{1,0:T(8,128)(2,1)}) %reduce-scatter.17.cloned.1.call-update) | async-done | bytes 1048592 | tf_op jit(solution)/shard_map/reduce_scatter | solution.py:255
  998.5 128.1 %reduce-scatter.23.cloned.1.call-done = bf16[512,2048]{0,1:T(8,128)(2,1)} async-done(((bf16[2048,2048]{0,1:T(8,128)(2,1)}), bf16[512,2048]{0,1:T(8,128)(2,1)}) %reduce-scatter.23.cloned.1.call-update) | async-done | bytes 2097168 | tf_op jit(solution)/shard_map/reduce_scatter | solution.py:208
  1137.4 60.2 %psum.14 = f32[]{:T(128)} all-reduce(f32[]{:T(128)} %get-tuple-element.22), channel_id=1, replica_groups=mesh['seq'=4,'wsh'=8] {'seq','wsh'}, use_global_device_ids=true, to_apply=%region_11.12 | all-reduce | flops 1 | bytes 8 | tf_op jit(solution)/shard_map/psum | solution.py:195
  1213.6 53.7 %reduce-scatter.25.cloned.1.call-done = f32[64,12]{1,0:T(8,128)} async-done(((f32[2048,12]{1,0:T(8,128)}), f32[64,12]{1,0:T(8,128)}) %reduce-scatter.25.cloned.1.call-update) | async-done | bytes 3088
  1268.3 60.1 %reduce-scatter.19.cloned.1.call-done = bf16[4,1,64,1536]{3,2,0,1:T(8,128)(2,1)} async-done(((bf16[4,8,64,1536]{3,2,0,1:T(8,128)(2,1)}), bf16[4,1,64,1536]{3,2,0,1:T(8,128)(2,1)}) %reduce-scatter.19.cloned.1.call-update) | async-done | bytes 786448 | tf_op jit(solution)/shard_map/reduce_scatter | solution.py:260
  (250 shorter events, 253.1 us)
Async XLA Ops:
  7.2 102.2 %all-gather.21.cloned.1.call-start = ((), (), s32[]{:S(2)}) async-start(), calls=%async_computation.24 | async-start | bytes 5242880 | tf_op jit(solution)/shard_map/all_gather | solution.py:123
  7.9 144.5 %all-gather.23.cloned.1.call-start = ((), (), s32[]{:S(2)}) async-start(), calls=%async_computation.25 | async-start | bytes 7077888 | tf_op jit(solution)/shard_map/all_gather | solution.py:129
  10.5 95.4 %copy-start.30 = (s32[1,1024]{1,0:T(1,128)S(1)}, s32[1,1024]{1,0:T(1,128)}, u32[]{:S(2)}) copy-start(s32[1,1024]{1,0:T(1,128)} %param.15) | copy-start | bytes 12292
  56.8 155.9 %all-gather.11.cloned.1.call-start = ((), (), s32[]{:S(2)}) async-start(), calls=%async_computation.12 | async-start | bytes 2359296 | tf_op jit(solution)/shard_map/all_gather | solution.py:131
  57.6 238.4 %reduce-scatter.11.cloned.1.call-start = ((), (), s32[]{:S(2)}) async-start(), calls=%async_computation.13 | async-start | bytes 5242880 | tf_op jit(solution)/shard_map/reduce_scatter | solution.py:176
  105.8 65.7 %copy-start.26 = (f32[2048,1]{0,1:T(1,128)}, f32[2048,1]{0,1:T(1,128)S(1)}, u32[]{:S(2)}) copy-start(f32[2048,1]{0,1:T(1,128)S(1)} %get-tuple-element.50) | copy-start | bytes 24580
  105.8 65.7 %copy-start.33 = (f32[2048,1]{0,1:T(1,128)}, f32[2048,1]{0,1:T(1,128)S(1)}, u32[]{:S(2)}) copy-start(f32[2048,1]{0,1:T(1,128)S(1)} %get-tuple-element.57) | copy-start | bytes 24580
  112.9 58.7 %copy-start.31 = (f32[1024]{0:T(1024)}, f32[1024]{0:T(1024)S(1)}, u32[]{:S(2)}) copy-start(f32[1024]{0:T(1024)S(1)} %broadcast_multiply_fusion) | copy-start | bytes 12292
  219.1 229.1 %all-gather.15.cloned.1.call-start = ((), (), s32[]{:S(2)}) async-start(), calls=%async_computation.15 | async-start | bytes 10485760 | tf_op jit(solution)/shard_map/all_gather | solution.py:137
  261.5 241.5 %all-gather.13.cloned.1.call-start = ((), (), s32[]{:S(2)}) async-start(), calls=%async_computation.14 | async-start | bytes 9437184 | tf_op jit(solution)/shard_map/all_gather | solution.py:183
  301.2 305.5 %reduce-scatter.13.cloned.1.call-start = ((), (), s32[]{:S(2)}) async-start(), calls=%async_computation.16 | async-start | bytes 9437184 | tf_op jit(solution)/shard_map/reduce_scatter | solution.py:188
  534.4 72.3 %copy-start.6 = (bf16[1,256,2048]{2,1,0:T(8,128)(2,1)S(1)}, bf16[1,256,2048]{2,1,0:T(8,128)(2,1)}, u32[]{:S(2)}) copy-start(bf16[1,256,2048]{2,1,0:T(8,128)(2,1)} %param.14) | copy-start | bytes 3145732
  534.5 130.8 %all-gather.17.cloned.1.call-start = ((), (), s32[]{:S(2)}) async-start(), calls=%async_computation.17 | async-start | bytes 9437184 | tf_op jit(solution)/shard_map/all_gather | solution.py:200
  610.9 160.9 %reduce-scatter.15.cloned.1.call-start = ((), (), s32[]{:S(2)}) async-start(), calls=%async_computation.18 | async-start | bytes 9437184 | tf_op jit(solution)/shard_map/reduce_scatter | solution.py:203
  700.1 160.5 %all-gather.19.cloned.1.call-start = ((), (), s32[]{:S(2)}) async-start(), calls=%async_computation.19 | async-start | bytes 5242880 | tf_op jit(solution)/shard_map/all_gather | solution.py:222
  779.7 199.5 %reduce-scatter.17.cloned.1.call-start = ((), (), s32[]{:S(2)}) async-start(), calls=%async_computation.20 | async-start | bytes 5242880 | tf_op jit(solution)/shard_map/reduce_scatter | solution.py:255
  780.3 85.7 %copy-start.11 = (bf16[1024,1,4,128]{0,3,2,1:T(8,128)(2,1)S(1)}, bf16[1024,1,4,128]{0,3,2,1:T(8,128)(2,1)}, u32[]{:S(2)}) copy-start(bf16[1024,1,4,128]{0,3,2,1:T(8,128)(2,1)} %copy-done.10) | copy-start | bytes 3145732
  903.8 222.8 %reduce-scatter.23.cloned.1.call-start = ((), (), s32[]{:S(2)}) async-start(), calls=%async_computation.23 | async-start | bytes 10485760 | tf_op jit(solution)/shard_map/reduce_scatter | solution.py:208
  942.8 324.6 %reduce-scatter.25.cloned.1.call-start = ((), (), s32[]{:S(2)}) async-start(), calls=%async_computation.26 | async-start | bytes 1081344
  983.2 345.2 %reduce-scatter.19.cloned.1.call-start = ((), (), s32[]{:S(2)}) async-start(), calls=%async_computation.21 | async-start | bytes 7077888 | tf_op jit(solution)/shard_map/reduce_scatter | solution.py:260
  1132.3 66.0 %all-to-all-start.3 = ((bf16[8,64,2,1024]{3,2,1,0:T(2,128)(2,1)}), bf16[8,64,2,1024]{3,2,1,0:T(2,128)(2,1)S(1)}, u32[]{:S(2)}, u32[]{:S(2)}) async-start(bf16[8,64,2,1024]{3,2,1,0:T(2,128)(2,1)} %reshape.344), calls=%async_computation.10 | async-start | bytes 4194304 | tf_op jit(solution)/shard_map/all_to_all | solution.py:211
  1136.0 237.2 %reduce-scatter.21.cloned.1.call-start = ((), (), s32[]{:S(2)}) async-start(), calls=%async_computation.22 | async-start | bytes 2359296 | tf_op jit(solution)/shard_map/reduce_scatter | solution.py:268
  1268.2 81.2 %copy-start.29 = (f32[64,12]{0,1:T(8,128)}, f32[64,12]{0,1:T(8,128)S(1)}, u32[]{:S(2)}) copy-start(f32[64,12]{0,1:T(8,128)S(1)} %copy.234) | copy-start | bytes 9220
  1332.1 24.7 %all-to-all-start.2 = ((bf16[4,64,3,512]{3,1,2,0:T(8,128)(2,1)}), bf16[4,64,3,512]{3,1,2,0:T(8,128)(2,1)S(1)}, u32[]{:S(2)}, u32[]{:S(2)}) async-start(bf16[4,64,3,512]{3,1,2,0:T(8,128)(2,1)} %copy.219), calls=%async_computation.7 | async-start | bytes 1572864 | tf_op jit(solution)/shard_map/all_to_all | solution.py:266
  (40 other events, 462.7 us)
Sparse Core Ops, SparseCore 0:
  9.6 95.6 all-gather.20
  107.7 44.6 all-gather.22
  154.3 27.7 all-gather.10
  219.2 76.7 reduce-scatter.10
  298.0 150.1 all-gather.14
  450.5 52.4 all-gather.12
  534.6 72.0 reduce-scatter.12
  611.0 54.2 all-gather.16
  700.2 71.4 reduce-scatter.14
  779.8 80.7 all-gather.18
  904.0 75.2 reduce-scatter.16
  981.5 145.1 reduce-scatter.22
  1129.5 137.8 reduce-scatter.24
  1270.6 57.7 reduce-scatter.18
  1332.0 41.0 reduce-scatter.20

commit v2 on v1

v2 whole, which is shorter than its diff:
```python
import functools
import math

import jax
import jax.numpy as jnp
from jax import lax
from jax.experimental import pallas as pl
from jax.experimental.pallas import tpu as pltpu
from jax.sharding import PartitionSpec as P

D = 2048
H = 16
DH = 128
FF = 8192
QBLK = 512
UPC = 4

eps_norm = 1e-05
beta_one = 0.9
beta_two = 0.95
adam_eps = 1e-08
decay_rate = 0.1
learn_rate = 0.05
gelu_coef = 0.7978845608028654
BF = jnp.bfloat16
F32 = jnp.float32


def norm_stats(value):
    row_mean = jnp.mean(value, axis=-1, keepdims=True)
    centred = value - row_mean
    variance = jnp.mean(centred * centred, axis=-1, keepdims=True)
    scale = lax.rsqrt(variance + eps_norm)
    return centred * scale, scale


def norm_back(grad, gain, hat, scale):
    e = grad * gain
    return scale * (
        e
        - jnp.mean(e, axis=-1, keepdims=True)
        - hat * jnp.mean(e * hat, axis=-1, keepdims=True)
    )


def gelu_tanh(value):
    return 0.5 * value * (1.0 + jnp.tanh(gelu_coef * (value + 0.044715 * value * value * value)))


def adam_update(weights, first, second, gradient, step_count):
    steps_done = step_count[0].astype(F32)
    first_new = beta_one * first + (1.0 - beta_one) * gradient
    second_new = beta_two * second + (1.0 - beta_two) * gradient * gradient
    fix_one = 1.0 - jnp.power(beta_one, steps_done)
    fix_two = 1.0 - jnp.power(beta_two, steps_done)
    update = first_new / fix_one / (jnp.sqrt(second_new / fix_two) + adam_eps)
    return (weights - learn_rate * (update + decay_rate * weights), first_new, second_new)


def contract_rows(left, right, out=F32):
    return lax.dot_general(
        left, right, (((0,), (0,)), ((), ())), preferred_element_type=F32
    ).astype(out)


def contract_cols(left, right, out=F32):
    return lax.dot_general(
        left, right, (((1,), (1,)), ((), ())), preferred_element_type=F32
    ).astype(out)


def dot(left, right):
    return jnp.dot(left, right, preferred_element_type=F32)


def block_scores(q_rows, key_rows, row_pos, key_pos, row_docs, key_docs, slopes, score_scale):
    scores = (
        jnp.einsum("qhd,khd->hqk", q_rows, key_rows, preferred_element_type=F32) * score_scale
    )
    distance = (row_pos[:, None] - key_pos[None, :]).astype(F32)
    scores = scores - slopes[:, None, None] * distance[None]
    allowed = (row_docs[:, None] == key_docs[None, :]) & (key_pos[None, :] <= row_pos[:, None])
    return jnp.where(allowed[None], scores, -jnp.inf)


def exchange_body(seq_size, wsh_size, spread, block_ref, out_ref, send_sems, recv_sems, own_sem):
    total = seq_size * wsh_size
    me = lax.axis_index("seq") * wsh_size + lax.axis_index("wsh")
    barrier = pltpu.get_barrier_semaphore()

    def place(index):
        return (index // wsh_size, index % wsh_size)

    def greet(step, carry):
        pl.semaphore_signal(
            barrier, inc=1, device_id=place((me + step) % total), device_id_type=pl.DeviceIdType.MESH
        )
        return carry

    lax.fori_loop(1, total, greet, 0)
    pl.semaphore_wait(barrier, total - 1)

    def copy(step):
        peer = (me + step) % total
        return pltpu.make_async_remote_copy(
            src_ref=block_ref.at[peer if spread else 0],
            dst_ref=out_ref.at[me],
            send_sem=send_sems.at[step],
            recv_sem=recv_sems.at[step],
            device_id=place(peer),
            device_id_type=pl.DeviceIdType.MESH,
        )

    own = pltpu.make_async_copy(block_ref.at[me if spread else 0], out_ref.at[me], own_sem)
    own.start()

    def start(step, carry):
        copy(step).start()
        return carry

    def finish(step, carry):
        copy(step).wait()
        return carry

    lax.fori_loop(1, total, start, 0)
    lax.fori_loop(1, total, finish, 0)
    own.wait()


def exchange_small(blocks, spread, seq_size, wsh_size, number):
    total = seq_size * wsh_size
    vmem = pl.BlockSpec(memory_space=pltpu.VMEM)
    return pl.pallas_call(
        functools.partial(exchange_body, seq_size, wsh_size, spread),
        out_shape=jax.ShapeDtypeStruct((total,) + blocks.shape[1:], blocks.dtype),
        in_specs=[vmem],
        out_specs=vmem,
        scratch_shapes=[
            pltpu.SemaphoreType.DMA((total,)),
            pltpu.SemaphoreType.DMA((total,)),
            pltpu.SemaphoreType.DMA,
        ],
        compiler_params=pltpu.CompilerParams(collective_id=number, has_side_effects=True),
    )(blocks)


def pack_tile(values):
    flat = values.reshape(values.shape[0], -1)
    width = -(-flat.shape[1] // 1024) * 1024
    flat = jnp.pad(flat, ((0, 0), (0, width - flat.shape[1])))
    return flat.reshape(values.shape[0], width // 128, 128)


def unpack_tile(tiles, shape):
    count = math.prod(shape)
    return tiles.reshape(tiles.shape[0], -1)[:, :count].reshape((tiles.shape[0],) + shape)


def ring_gather(rows, axis, size):
    half = rows.shape[0] // 2
    upper, lower = rows[:half], rows[half:]
    steps = [(upper, lower)]
    for _ in range(1, size):
        upper = lax.ppermute(upper, axis, [(i, (i + 1) % size) for i in range(size)])
        lower = lax.ppermute(lower, axis, [(i, (i - 1) % size) for i in range(size)])
        steps.append((upper, lower))
    return steps


def ring_scatter(steps, axis, size):
    upper, lower = steps[1]
    for k in range(2, size + 1):
        upper = lax.ppermute(upper, axis, [(i, (i + 1) % size) for i in range(size)])
        lower = lax.ppermute(lower, axis, [(i, (i - 1) % size) for i in range(size)])
        upper = upper.astype(F32) + steps[k % size][0].astype(F32)
        lower = lower.astype(F32) + steps[k % size][1].astype(F32)
        if k < size:
            upper, lower = upper.astype(BF), lower.astype(BF)
    return jnp.concatenate([upper, lower], axis=0)


def swap(value, mask, axis, size):
    return lax.ppermute(value, axis, [(i, i ^ mask) for i in range(size)])


def plane_gather(rows, axis, size):
    if size != 8:
        parts = lax.all_gather(rows, axis, axis=0)
        return [parts[i] for i in range(size)]
    half = rows.shape[0] // 2
    across = swap(rows, 2, axis, size)
    along = swap(rows, 4, axis, size)
    corner = jnp.concatenate(
        [swap(across[:half], 4, axis, size), swap(along[half:], 2, axis, size)], axis=0
    )
    blocks = []
    for block in (rows, across, along, corner):
        blocks += [block, swap(block, 1, axis, size)]
    return blocks


def plane_scatter(blocks, axis, size):
    if size != 8:
        return lax.psum_scatter(
            jnp.stack(blocks), axis, scatter_dimension=0, tiled=False
        ).astype(F32)
    half = blocks[0].shape[0] // 2

    def add(left, right):
        return (left.astype(F32) + right.astype(F32)).astype(BF)

    corner = add(blocks[6], swap(blocks[7], 1, axis, size))
    across = add(blocks[2], swap(blocks[3], 1, axis, size))
    along = add(blocks[4], swap(blocks[5], 1, axis, size))
    own = add(blocks[0], swap(blocks[1], 1, axis, size))
    along_upper = add(along[:half], swap(corner[:half], 2, axis, size))
    across_lower = add(across[half:], swap(corner[half:], 4, axis, size))
    across_sum = jnp.concatenate([across[:half], across_lower], axis=0)
    along_sum = jnp.concatenate([along_upper, along[half:]], axis=0)
    return (
        own.astype(F32)
        + swap(across_sum, 2, axis, size).astype(F32)
        + swap(along_sum, 4, axis, size).astype(F32)
    )


def shards(
    inputs,
    cotangent,
    teacher,
    document_ids,
    valid_flags,
    step_count,
    attn_params,
    attn_first,
    attn_second,
    mlp_params,
    mlp_first,
    mlp_second,
):
    tok_rows = inputs.shape[1]
    seq_size = lax.axis_size("seq")
    wsh_size = lax.axis_size("wsh")
    seq_at = lax.axis_index("seq")
    wsh_at = lax.axis_index("wsh")
    own_rows = attn_params.shape[0]
    seq_len = tok_rows * seq_size
    token_total = seq_len * wsh_size
    heads_here = H // seq_size
    head_cols = heads_here * DH
    ff_cols = FF // wsh_size
    score_scale = 1.0 / math.sqrt(DH)
    nblocks = seq_len // QBLK

    input_steps = ring_gather(inputs[0], "seq", seq_size)
    half_rows = tok_rows // 2
    group = QBLK // tok_rows

    def grouped(steps, index):
        parts = []
        for pair in steps[index * group : (index + 1) * group]:
            parts += list(pair)
        return jnp.concatenate(parts, axis=0)

    def ungrouped(blocks):
        steps = []
        for block in blocks:
            for k in range(group):
                base = k * tok_rows
                steps.append(
                    (block[base : base + half_rows], block[base + half_rows : base + tok_rows])
                )
        return steps

    starts = []
    for k in range(seq_size):
        starts.append(
            (
                ((seq_at - k) % seq_size) * tok_rows,
                ((seq_at + k) % seq_size) * tok_rows + half_rows,
            )
        )
    ramp = jnp.arange(half_rows, dtype=jnp.int32)
    row_pos = [grouped([(a + ramp, b + ramp) for a, b in starts], g) for g in range(nblocks)]
    doc_row = document_ids[0]
    doc_steps = [
        tuple(lax.dynamic_slice(doc_row, (at,), (half_rows,)) for at in pair) for pair in starts
    ]
    row_docs = [grouped(doc_steps, g) for g in range(nblocks)]
    key_pos = jnp.concatenate(row_pos)
    key_docs = jnp.concatenate(row_docs)

    valid_float = valid_flags[0].astype(F32)
    own_vectors = jnp.concatenate([attn_params[:, 4 * D :], mlp_params[:, 2 * FF :]], axis=1)
    own_vectors = own_vectors.astype(BF).astype(F32)
    count_column = jnp.zeros((own_rows, 1), F32).at[0, 0].set(jnp.sum(valid_float))
    arrived_vectors = exchange_small(
        pack_tile(jnp.concatenate([own_vectors, count_column], axis=1)[None]),
        False,
        seq_size,
        wsh_size,
        0,
    )
    vectors = unpack_tile(arrived_vectors, (own_rows, 13)).reshape(D, 13)
    valid_count = jnp.sum(vectors[:, 12])
    gain_one, shift_one, bias_query, bias_value, bias_dense = (vectors[:, i] for i in range(5))
    gain_two, shift_two = vectors[:, 5], vectors[:, 6]
    bias_up = vectors[:, 7 : 7 + UPC].T.reshape(FF)
    bias_down = vectors[:, 7 + UPC]

    attn_low = attn_params[:, : 4 * D].astype(BF)
    qkv_own = jnp.stack(
        [
            jnp.concatenate(
                [
                    attn_low[:, part * D + s * head_cols : part * D + (s + 1) * head_cols]
                    for part in range(3)
                ],
                axis=1,
            )
            for s in range(seq_size)
        ]
    )
    qkv_cols = lax.all_to_all(qkv_own, "seq", split_axis=0, concat_axis=0, tiled=True)
    w_qkv = lax.all_gather(qkv_cols, "wsh", axis=1)
    w_qkv = w_qkv.reshape(D, 3 * head_cols)
    w_dense = lax.all_gather(attn_low[:, 3 * D :], "wsh", axis=0, tiled=True)

    mlp_low = mlp_params[:, : 2 * FF].astype(BF)
    mlp_own = jnp.stack(
        [
            jnp.concatenate(
                [mlp_low[:, part * FF + w * ff_cols : part * FF + (w + 1) * ff_cols] for part in range(2)],
                axis=1,
            )
            for w in range(wsh_size)
        ]
    )
    mlp_cols = lax.all_to_all(mlp_own, "wsh", split_axis=0, concat_axis=0, tiled=True)
    mlp_cols = mlp_cols.reshape(wsh_size * own_rows, 2 * ff_cols)
    w_up = lax.all_gather(mlp_cols[:, :ff_cols], "seq", axis=0, tiled=True)
    w_down_t = lax.all_gather(mlp_cols[:, ff_cols:], "seq", axis=0, tiled=True)

    acts = inputs[0].astype(F32)
    hat_one, scale_one = norm_stats(acts)
    bias_q = lax.dynamic_slice(bias_query, (seq_at * head_cols,), (head_cols,))
    bias_v = lax.dynamic_slice(bias_value, (seq_at * head_cols,), (head_cols,))
    qkv_bias = jnp.concatenate([bias_q, jnp.zeros_like(bias_q), bias_v])
    normed_blocks = []
    projected_blocks = []
    for g in range(nblocks):
        rows = grouped(input_steps, g).astype(F32)
        normed_blocks.append((norm_stats(rows)[0] * gain_one + shift_one).astype(BF))
        projected_blocks.append(
            (dot(normed_blocks[g], w_qkv) + qkv_bias).astype(BF).reshape(QBLK, 3, heads_here, DH)
        )
    queries = [block[:, 0] for block in projected_blocks]
    keys_all = jnp.concatenate([block[:, 1] for block in projected_blocks], axis=0)
    values = jnp.concatenate([block[:, 2] for block in projected_blocks], axis=0)
    head_ids = seq_at * heads_here + jnp.arange(heads_here, dtype=jnp.int32)
    slopes = jnp.exp2(-8.0 * (head_ids.astype(F32) + 1.0) / H)
    attended_blocks = []
    log_blocks = []
    dense_blocks = []
    for g in range(nblocks):
        scores = block_scores(
            queries[g], keys_all, row_pos[g], key_pos, row_docs[g], key_docs, slopes, score_scale
        )
        row_top = jnp.max(scores, axis=-1, keepdims=True)
        exp_scores = jnp.exp(scores - row_top)
        row_total = jnp.sum(exp_scores, axis=-1, keepdims=True)
        prob_low = (exp_scores / row_total).astype(BF)
        log_blocks.append(row_top + jnp.log(row_total))
        block_out = jnp.einsum("hqk,khd->qhd", prob_low, values, preferred_element_type=F32)
        attended_blocks.append(block_out.astype(BF).reshape(QBLK, head_cols))
        dense_blocks.append(dot(attended_blocks[g], w_dense).astype(BF))
    dense_out = ring_scatter(ungrouped(dense_blocks), "seq", seq_size)
    middle = acts + dense_out + bias_dense

    hat_two, scale_two = norm_stats(middle)
    normed_two_low = (hat_two * gain_two + shift_two).astype(BF)
    normed_two_parts = plane_gather(normed_two_low, "wsh", wsh_size)
    bias_up_here = lax.dynamic_slice(bias_up, (wsh_at * ff_cols,), (ff_cols,))
    upper_parts = [dot(part, w_up) + bias_up_here for part in normed_two_parts]
    active_parts = [gelu_tanh(part).astype(BF) for part in upper_parts]
    down_out = plane_scatter(
        [contract_cols(part, w_down_t, BF) for part in active_parts], "wsh", wsh_size
    )
    result = middle + down_out + bias_down

    cot_float = cotangent[0].astype(F32)
    deviation = result - teacher[0].astype(F32)
    squared_part = jnp.sum(valid_float[:, None] * deviation * deviation)
    result_grad = cot_float + valid_float[:, None] * (token_total / valid_count) * deviation
    down_grad = result_grad.astype(BF)

    down_grad_parts = plane_gather(down_grad, "wsh", wsh_size)
    upper_low_parts = []
    for grad_part, upper_part in zip(down_grad_parts, upper_parts):
        gelu_back = jax.vjp(gelu_tanh, upper_part)[1]
        (upper_grad,) = gelu_back(dot(grad_part, w_down_t))
        upper_low_parts.append(upper_grad.astype(BF))
    normed_two_grad = plane_scatter(
        [contract_cols(part, w_up, BF) for part in upper_low_parts], "wsh", wsh_size
    )
    upper_low = jnp.concatenate(upper_low_parts, axis=0)
    down_part = contract_rows(
        jnp.concatenate(down_grad_parts, axis=0), jnp.concatenate(active_parts, axis=0), BF
    )
    up_part = contract_rows(jnp.concatenate(normed_two_parts, axis=0), upper_low, BF)

    def mlp_rows(part):
        rows = lax.psum_scatter(part, "seq", scatter_dimension=0, tiled=True)
        rows = lax.all_to_all(
            rows.reshape(wsh_size, own_rows, ff_cols), "wsh", split_axis=0, concat_axis=0, tiled=True
        )
        return [rows[w] for w in range(wsh_size)]

    down_rows = mlp_rows(down_part)
    up_rows = mlp_rows(up_part)
    mlp_gradient = jnp.concatenate(up_rows + down_rows, axis=1).astype(F32)
    middle_grad = result_grad + norm_back(normed_two_grad, gain_two, hat_two, scale_two)

    dense_grad = middle_grad.astype(BF)
    grad_steps = ring_gather(dense_grad, "seq", seq_size)
    key_grad = jnp.zeros((seq_len, heads_here, DH), F32)
    value_grad = jnp.zeros((seq_len, heads_here, DH), F32)
    grad_blocks = []
    query_blocks = []
    for g in range(nblocks):
        grad_blocks.append(grouped(grad_steps, g))
        q_rows = queries[g]
        grad_rows = contract_cols(grad_blocks[g], w_dense, BF).reshape(QBLK, heads_here, DH)
        scores = block_scores(
            q_rows, keys_all, row_pos[g], key_pos, row_docs[g], key_docs, slopes, score_scale
        )
        prob = jnp.exp(scores - log_blocks[g])
        prob_low = prob.astype(BF)
        prob_grad = jnp.einsum("qhd,khd->hqk", grad_rows, values, preferred_element_type=F32)
        row_delta = jnp.sum(prob * prob_grad, axis=-1, keepdims=True)
        score_grad = (prob * (prob_grad - row_delta)).astype(BF)
        query_blocks.append(
            jnp.einsum("hqk,khd->qhd", score_grad, keys_all, preferred_element_type=F32)
            * score_scale
        )
        key_grad = key_grad + (
            jnp.einsum("hqk,qhd->khd", score_grad, q_rows, preferred_element_type=F32)
            * score_scale
        )
        value_grad = value_grad + jnp.einsum(
            "hqk,qhd->khd", prob_low, grad_rows, preferred_element_type=F32
        )
    query_grad = jnp.concatenate(query_blocks, axis=0)
    projected_grad = jnp.concatenate(
        [
            part.astype(BF).reshape(seq_len, head_cols)
            for part in (query_grad, key_grad, value_grad)
        ],
        axis=1,
    )
    normed_blocks_grad = [
        contract_cols(projected_grad[g * QBLK : (g + 1) * QBLK], w_qkv, BF) for g in range(nblocks)
    ]
    normed_grad = ring_scatter(ungrouped(normed_blocks_grad), "seq", seq_size)
    input_grad = middle_grad + norm_back(normed_grad, gain_one, hat_one, scale_one)
    dense_part = contract_rows(
        jnp.concatenate(attended_blocks, axis=0), jnp.concatenate(grad_blocks, axis=0), BF
    )
    qkv_part = contract_rows(jnp.concatenate(normed_blocks, axis=0), projected_grad, BF)
    qkv_rows = lax.psum_scatter(
        qkv_part.reshape(seq_size, wsh_size, own_rows, 3 * head_cols),
        "wsh",
        scatter_dimension=1,
        tiled=True,
    ).reshape(seq_size, own_rows, 3 * head_cols)
    qkv_gradient = lax.all_to_all(qkv_rows, "seq", split_axis=0, concat_axis=0, tiled=True)
    qkv_gradient = [
        qkv_gradient[s, :, part * head_cols : (part + 1) * head_cols]
        for part in range(3)
        for s in range(seq_size)
    ]
    dense_gradient = lax.psum_scatter(dense_part, "wsh", scatter_dimension=0, tiled=True)
    attn_gradient = jnp.concatenate(qkv_gradient + [dense_gradient], axis=1).astype(F32)

    zeros = jnp.zeros((D,), F32)
    qkv_sums = jnp.sum(projected_grad, axis=0, dtype=F32)
    query_sums = lax.dynamic_update_slice(zeros, qkv_sums[:head_cols], (seq_at * head_cols,))
    value_sums = lax.dynamic_update_slice(zeros, qkv_sums[2 * head_cols :], (seq_at * head_cols,))
    up_sums = lax.dynamic_update_slice(
        jnp.zeros((FF,), F32), jnp.sum(upper_low, axis=0, dtype=F32), (wsh_at * ff_cols,)
    )
    vector_part = jnp.concatenate(
        [
            jnp.stack(
                [
                    jnp.sum(normed_grad * hat_one, axis=0),
                    jnp.sum(normed_grad, axis=0),
                    query_sums,
                    value_sums,
                    jnp.sum(dense_grad, axis=0, dtype=F32),
                    jnp.sum(normed_two_grad * hat_two, axis=0),
                    jnp.sum(normed_two_grad, axis=0),
                ],
                axis=1,
            ),
            up_sums.reshape(UPC, D).T,
            jnp.sum(down_grad, axis=0, dtype=F32)[:, None],
            jnp.full((D, 1), squared_part, F32),
        ],
        axis=1,
    )
    arrived_parts = exchange_small(
        pack_tile(vector_part.reshape(seq_size * wsh_size, own_rows, 13)),
        True,
        seq_size,
        wsh_size,
        1,
    )
    vector_sums = unpack_tile(jnp.sum(arrived_parts, axis=0)[None], (own_rows, 13))[0]
    vector_gradient = vector_sums[:, :12]
    losses = jnp.stack([vector_sums[0, 12] / (valid_count * D)])
    attn_gradient = jnp.concatenate([attn_gradient, vector_gradient[:, :5]], axis=1)
    mlp_gradient = jnp.concatenate([mlp_gradient, vector_gradient[:, 5:]], axis=1)
    attn_new, attn_first_new, attn_second_new = adam_update(
        attn_params, attn_first, attn_second, attn_gradient, step_count
    )
    mlp_new, mlp_first_new, mlp_second_new = adam_update(
        mlp_params, mlp_first, mlp_second, mlp_gradient, step_count
    )
    return (
        result.astype(BF)[None],
        losses,
        input_grad[None],
        vector_gradient,
        attn_new,
        attn_first_new,
        attn_second_new,
        mlp_new,
        mlp_first_new,
        mlp_second_new,
    )


def solution(mesh):
    rows = P(("seq", "wsh"), None)
    tokens = P("wsh", "seq", None)
    return jax.shard_map(
        shards,
        mesh=mesh,
        in_specs=(tokens, tokens, tokens, P("wsh", None), P("wsh", "seq"), P()) + (rows,) * 6,
        out_specs=(tokens, P(), tokens) + (rows,) * 7,
        check_vma=False,
    )
```

time: 1390 us -> 1000 us (0.72)
  waiting for transfers between devices: 809 us -> 473 us
  blocking collectives: 220 us -> 26.4 us
  starting transfers between devices: 9.67 us -> 79.1 us
  Pallas kernels: 0 us -> 20 us
  other arithmetic: 74.2 us -> 93.3 us
  matrix products: 170 us -> 187 us
    ppermute x0 -> x56, waiting for transfers between devices: none -> 423 us  [the longest x6 101 us: ring_gather(): lax.ppermute(lower, axis, [(i, (i - 1) % size) for i in range(size)])]
    all_gather x6 -> x3, waiting for transfers between devices: 336 us -> 0.01 us  [the longest x1 0.01 us: shards(): w_dense = lax.all_gather(attn_low[:, 3 * D:], 'wsh', axis=0, tiled=True)]
    reduce_scatter x5 -> x2, waiting for transfers between devices: 300 us -> 0.02 us  [mlp_rows(): rows = lax.psum_scatter(part, 'seq', scatter_dimension=0, tiled=True)]
    psum x2 -> x0, blocking collectives: 101 us -> none  [the longest x1 60.2 us: shards(): lax.psum(jnp.sum(valid_float[:, None] * deviation * deviation), ('seq', '...]
    ppermute x0 -> x56, starting transfers between devices: none -> 62.2 us  [the longest x32 20.8 us: swap(): return lax.ppermute(value, axis, [(i, i ^ mask) for i in range(size)])]
    reduce_scatter x1, waiting for transfers between devices: 60.1 us -> 0.01 us  [shards(): lax.psum_scatter(qkv_part.reshape(seq_size, wsh_size, own_rows, 3 * head_...]
    unnamed x16 -> x8, waiting for transfers between devices: 54.6 us -> 0.13 us
    all_to_all x2 -> x1, blocking collectives: 73.9 us -> 26.4 us  [shards(): lax.all_to_all(qkv_own, 'seq', split_axis=0, concat_axis=0, tiled=True)]
  transfers between devices with their start and end apart: 17 -> 68, of which waited for: 14 -> 37; matrix products, arithmetic and copies ran while one was open for 14% -> 35% of each run, Pallas kernels for 0% -> 2%
where the time goes in v2:
time: 1000 us; the launch traced here: 992 us
  waiting for transfers between devices  473 us (47%)
  matrix products  187 us (19%)
  local copies, waits for them, and re-layouts  93.5 us (9%)
  other arithmetic  93.3 us (9%)
  starting transfers between devices  79.1 us (8%)
  blocking collectives  26.4 us (3%)
  between operations  20.8 us (2%)
  Pallas kernels  20 us (2%)
    ppermute x6, waiting for transfers between devices, ring_gather(): lax.ppermute(lower, axis, [(i, (i - 1) % size) for i in range(size)])  101 us
    ppermute x32, waiting for transfers between devices, swap(): return lax.ppermute(value, axis, [(i, i ^ mask) for i in range(size)])  99.9 us
    ppermute x6, waiting for transfers between devices, ring_scatter(): lax.ppermute(upper, axis, [(i, (i + 1) % size) for i in range(size)])  87.8 us
    ppermute x6, waiting for transfers between devices, ring_scatter(): lax.ppermute(lower, axis, [(i, (i - 1) % size) for i in range(size)])  78.3 us
    dot_general x20, matrix products, dot(): return jnp.dot(left, right, preferred_element_type=F32)  64.6 us
    dot_general x20, matrix products, contract_cols(): lax.dot_general(left, right, (((1,), (1,)), ((), ())), preferred_element_...  56.3 us
    ppermute x6, waiting for transfers between devices, ring_gather(): lax.ppermute(upper, axis, [(i, (i + 1) % size) for i in range(size)])  55.9 us
    unnamed x284, local copies, waits for them, and re-layouts  52 us
  transfers between devices with their start and end apart: 68, of which 37 were waited for; matrix products, arithmetic and copies ran while one was open for 35% of the time, Pallas kernels for 2%

profile of v2, /device:TPU:0, one launch (start us, length us, event | category | flops | bytes accessed | tf_op | source)
XLA Modules:
  0.0 992.4 jit_solution(6932853854441481463)
XLA Ops:
  9.2 26.4 %all_to_all.25 = bf16[4,64,1536]{2,1,0:T(8,128)(2,1)} all-to-all(bf16[4,64,1536]{2,1,0:T(8,128)(2,1)S(1)} %pad_maximum_fusion.12), channel_id=1, replica_groups=mesh['seq'=4,'wsh'=8] {'seq'}, dimensions={0} | all-to-all | bytes 1572864 | tf_op jit(solution)/shard_map/all_to_all | solution.py:324
  55.7 26.7 %all-to-all-done.1 = bf16[8,64,2048]{2,1,0:T(8,128)(2,1)} async-done(((bf16[8,64,2048]{2,1,0:T(8,128)(2,1)}), bf16[8,64,2048]{2,1,0:T(8,128)(2,1)}, u32[]{:S(2)}, u32[]{:S(2)}) %all-to-all-start.1) | async-done | bytes 2097184 | tf_op jit(solution)/shard_map/all_to_all | solution.py:339
  86.5 10.0 %shard_map.195 = f32[32,8,128]{2,1,0:T(8,128)} custom-call(f32[1,8,128]{2,1,0:T(8,128)} %bitcast.436), custom_call_target="tpu_custom_call" | custom-call | tf_op jit(solution)/shard_map/pallas_call | solution.py:133
  114.9 11.1 %collective-permute-done.2 = bf16[128,2048]{1,0:T(8,128)(2,1)S(1)} collective-permute-done((bf16[128,2048]{1,0:T(8,128)(2,1)}, bf16[128,2048]{1,0:T(8,128)(2,1)S(1)}, u32[]{:S(2)}, u32[]{:S(2)}) %collective-permute-start.2) | collective-permute-done | bytes 524320 | tf_op jit(solution)/shard_map/ppermute | solution.py:164
  126.1 10.0 %collective-permute-done.3 = bf16[128,2048]{1,0:T(8,128)(2,1)S(1)} collective-permute-done((bf16[128,2048]{1,0:T(8,128)(2,1)}, bf16[128,2048]{1,0:T(8,128)(2,1)S(1)}, u32[]{:S(2)}, u32[]{:S(2)}) %collective-permute-start.3) | collective-permute-done | bytes 524320 | tf_op jit(solution)/shard_map/ppermute | solution.py:165
  141.4 18.8 %collective-permute-done.4 = bf16[128,2048]{1,0:T(8,128)(2,1)S(1)} collective-permute-done((bf16[128,2048]{1,0:T(8,128)(2,1)S(1)}, bf16[128,2048]{1,0:T(8,128)(2,1)S(1)}, u32[]{:S(2)}, u32[]{:S(2)}) %collective-permute-start.4) | collective-permute-done | bytes 524320 | tf_op jit(solution)/shard_map/ppermute | solution.py:164
  160.1 21.4 %collective-permute-done.5 = bf16[128,2048]{1,0:T(8,128)(2,1)S(1)} collective-permute-done((bf16[128,2048]{1,0:T(8,128)(2,1)S(1)}, bf16[128,2048]{1,0:T(8,128)(2,1)S(1)}, u32[]{:S(2)}, u32[]{:S(2)}) %collective-permute-start.5) | collective-permute-done | bytes 524320 | tf_op jit(solution)/shard_map/ppermute | solution.py:165
  254.3 14.3 %collective-permute-done.6 = bf16[128,2048]{1,0:T(8,128)(2,1)S(1)} collective-permute-done((bf16[128,2048]{1,0:T(8,128)(2,1)S(1)}, bf16[128,2048]{1,0:T(8,128)(2,1)S(1)}, u32[]{:S(2)}, u32[]{:S(2)}) %collective-permute-start.6) | collective-permute-done | bytes 524320 | tf_op jit(solution)/shard_map/ppermute | solution.py:173
  268.6 22.2 %collective-permute-done.9 = bf16[128,2048]{1,0:T(8,128)(2,1)S(1)} collective-permute-done((bf16[128,2048]{1,0:T(8,128)(2,1)S(1)}, bf16[128,2048]{1,0:T(8,128)(2,1)S(1)}, u32[]{:S(2)}, u32[]{:S(2)}) %collective-permute-start.9) | collective-permute-done | bytes 524320 | tf_op jit(solution)/shard_map/ppermute | solution.py:174
  295.1 24.0 %collective-permute-done.7 = bf16[128,2048]{1,0:T(8,128)(2,1)S(1)} collective-permute-done((bf16[128,2048]{1,0:T(8,128)(2,1)S(1)}, bf16[128,2048]{1,0:T(8,128)(2,1)S(1)}, u32[]{:S(2)}, u32[]{:S(2)}) %collective-permute-start.7) | collective-permute-done | bytes 524320 | tf_op jit(solution)/shard_map/ppermute | solution.py:173
  319.1 22.0 %collective-permute-done.10 = bf16[128,2048]{1,0:T(8,128)(2,1)S(1)} collective-permute-done((bf16[128,2048]{1,0:T(8,128)(2,1)S(1)}, bf16[128,2048]{1,0:T(8,128)(2,1)S(1)}, u32[]{:S(2)}, u32[]{:S(2)}) %collective-permute-start.10) | collective-permute-done | bytes 524320 | tf_op jit(solution)/shard_map/ppermute | solution.py:174
  345.5 18.9 %collective-permute-done.8 = bf16[128,2048]{1,0:T(8,128)(2,1)S(1)} collective-permute-done((bf16[128,2048]{1,0:T(8,128)(2,1)S(1)}, bf16[128,2048]{1,0:T(8,128)(2,1)S(1)}, u32[]{:S(2)}, u32[]{:S(2)}) %collective-permute-start.8) | collective-permute-done | bytes 524320 | tf_op jit(solution)/shard_map/ppermute | solution.py:173
  383.0 18.3 %collective-permute-done.18 = bf16[256,2048]{1,0:T(8,128)(2,1)} collective-permute-done((bf16[256,2048]{1,0:T(8,128)(2,1)}, bf16[256,2048]{1,0:T(8,128)(2,1)}, u32[]{:S(2)}, u32[]{:S(2)}) %collective-permute-start.18) | collective-permute-done | bytes 1048608 | tf_op jit(solution)/shard_map/ppermute | solution.py:183
  453.6 10.6 %collective-permute-done.26 = bf16[128,2048]{1,0:T(8,128)(2,1)S(1)} collective-permute-done((bf16[128,2048]{1,0:T(8,128)(2,1)S(1)}, bf16[128,2048]{1,0:T(8,128)(2,1)S(1)}, u32[]{:S(2)}, u32[]{:S(2)}) %collective-permute-start.26) | collective-permute-done | bytes 524320 | tf_op jit(solution)/shard_map/ppermute | solution.py:183
  474.0 15.7 %collective-permute-done.27 = bf16[256,2048]{1,0:T(8,128)(2,1)S(1)} collective-permute-done((bf16[256,2048]{1,0:T(8,128)(2,1)S(1)}, bf16[256,2048]{1,0:T(8,128)(2,1)S(1)}, u32[]{:S(2)}, u32[]{:S(2)}) %collective-permute-start.27) | collective-permute-done | bytes 1048608 | tf_op jit(solution)/shard_map/ppermute | solution.py:183
  502.8 14.8 %collective-permute-done.34 = bf16[256,2048]{1,0:T(8,128)(2,1)S(1)} collective-permute-done((bf16[256,2048]{1,0:T(8,128)(2,1)S(1)}, bf16[256,2048]{1,0:T(8,128)(2,1)S(1)}, u32[]{:S(2)}, u32[]{:S(2)}) %collective-permute-start.34) | collective-permute-done | bytes 1048608 | tf_op jit(solution)/shard_map/ppermute | solution.py:183
  559.0 10.9 %convolution_convert_fusion.2 = bf16[2048,1024]{1,0:T(8,128)(2,1)} fusion(bf16[2048,2048]{1,0:T(8,128)(2,1)S(1)} %constant_dynamic-update-slice_fusion.34, bf16[2048,1024]{1,0:T(8,128)(2,1)S(1)} %get-tuple-element.168), kind=kOutput, calls=%fused_computation.50 | convolution fusion | flops 8592031744 | bytes 16777216 | tf_op jit(solution)/shard_map/dot_general | solution.py:61
  602.3 18.2 %collective-permute-done.43 = bf16[256,2048]{1,0:T(8,128)(2,1)S(1)} collective-permute-done((bf16[256,2048]{1,0:T(8,128)(2,1)S(1)}, bf16[256,2048]{1,0:T(8,128)(2,1)S(1)}, u32[]{:S(2)}, u32[]{:S(2)}) %collective-permute-start.43) | collective-permute-done | bytes 1048608 | tf_op jit(solution)/shard_map/ppermute | solution.py:183
  634.2 10.9 %convolution_convert_fusion.1 = bf16[2048,1024]{1,0:T(8,128)(2,1)} fusion(bf16[2048,2048]{1,0:T(8,128)(2,1)S(1)} %constant_dynamic-update-slice_fusion.43, bf16[2048,1024]{1,0:T(8,128)(2,1)S(1)} %copy-done.97), kind=kOutput, calls=%fused_computation.49 | convolution fusion | flops 8592031744 | bytes 16777216 | tf_op jit(solution)/shard_map/dot_general | solution.py:61
  645.2 13.1 %collective-permute-done.44 = bf16[128,2048]{1,0:T(8,128)(2,1)} collective-permute-done((bf16[128,2048]{1,0:T(8,128)(2,1)}, bf16[128,2048]{1,0:T(8,128)(2,1)}, u32[]{:S(2)}, u32[]{:S(2)}) %collective-permute-start.44) | collective-permute-done | bytes 524320 | tf_op jit(solution)/shard_map/ppermute | solution.py:164
  687.5 33.4 %collective-permute-done.47 = bf16[128,2048]{1,0:T(8,128)(2,1)S(1)} collective-permute-done((bf16[128,2048]{1,0:T(8,128)(2,1)}, bf16[128,2048]{1,0:T(8,128)(2,1)S(1)}, u32[]{:S(2)}, u32[]{:S(2)}) %collective-permute-start.47) | collective-permute-done | bytes 524320 | tf_op jit(solution)/shard_map/ppermute | solution.py:165
  732.4 27.1 %collective-permute-done.49 = bf16[128,2048]{1,0:T(8,128)(2,1)S(1)} collective-permute-done((bf16[128,2048]{1,0:T(8,128)(2,1)S(1)}, bf16[128,2048]{1,0:T(8,128)(2,1)S(1)}, u32[]{:S(2)}, u32[]{:S(2)}) %collective-permute-start.49) | collective-permute-done | bytes 524320 | tf_op jit(solution)/shard_map/ppermute | solution.py:165
  840.8 12.6 %collective-permute-done.51 = bf16[128,2048]{1,0:T(8,128)(2,1)S(1)} collective-permute-done((bf16[128,2048]{1,0:T(8,128)(2,1)S(1)}, bf16[128,2048]{1,0:T(8,128)(2,1)S(1)}, u32[]{:S(2)}, u32[]{:S(2)}) %collective-permute-start.51) | collective-permute-done | bytes 524320 | tf_op jit(solution)/shard_map/ppermute | solution.py:173
  950.9 11.5 %multiply_subtract_fusion = (f32[64,16391]{1,0:T(8,128)}, f32[64,16391]{1,0:T(8,128)}, f32[64,16391]{1,0:T(8,128)}) fusion(f32[64,16391]{1,0:T(8,128)} %param.23, f32[]{:T(128)} %bitcast.82, f32[]{:T(128)} %bitcast.81, f32[64,7]{1,0:T(8,128)S(1)} %slice.675, f32[64,16384]{1,0:T(8,128)} %convert_element_type.667, f32[64,16391]{1,0:T(8,128)} %param.25, ...), kind=kLoop, calls=%fused_computation.30 | loop fusion | flops 16784384 | bytes 29372680 | tf_op jit(solution)/shard_map/sub | solution.py:57
  (628 shorter events, 548.7 us)
Async XLA Ops:
  7.2 184.5 %all-gather.12.cloned.1.call-start = ((), (), s32[]{:S(2)}) async-start(), calls=%async_computation.16 | async-start | bytes 7077888 | tf_op jit(solution)/shard_map/all_gather | solution.py:325
  35.6 201.8 %all-gather.6.cloned.1.call-start = ((), (), s32[]{:S(2)}) async-start(), calls=%async_computation.9 | async-start | bytes 2359296 | tf_op jit(solution)/shard_map/all_gather | solution.py:327
  44.9 37.5 %all-to-all-start.1 = ((bf16[8,64,2048]{2,1,0:T(8,128)(2,1)}), bf16[8,64,2048]{2,1,0:T(8,128)(2,1)}, u32[]{:S(2)}, u32[]{:S(2)}) async-start(bf16[8,64,2048]{2,1,0:T(8,128)(2,1)} %fusion.142), calls=%async_computation.1 | async-start | bytes 4194304 | tf_op jit(solution)/shard_map/all_to_all | solution.py:339
  49.3 359.2 %all-gather.8.cloned.1.call-start = ((), (), s32[]{:S(2)}) async-start(), calls=%async_computation.10 | async-start | bytes 5242880 | tf_op jit(solution)/shard_map/all_gather | solution.py:341
  50.4 58.8 %collective-permute-start = (bf16[128,2048]{1,0:T(8,128)(2,1)}, bf16[128,2048]{1,0:T(8,128)(2,1)}, u32[]{:S(2)}, u32[]{:S(2)}) collective-permute-start(bf16[128,2048]{1,0:T(8,128)(2,1)} %get-tuple-element.199), channel_id=1, source_target_pairs={{0,8},{8,16},{16,24},{24,0},{1,9},{9,17},{17,25},{25,1},{2,10},{10... | collective-permute-start | bytes 1572872 | tf_op jit(solution)/shard_map/ppermute | solution.py:164
  50.6 60.2 %collective-permute-start.1 = (bf16[128,2048]{1,0:T(8,128)(2,1)}, bf16[128,2048]{1,0:T(8,128)(2,1)}, u32[]{:S(2)}, u32[]{:S(2)}) collective-permute-start(bf16[128,2048]{1,0:T(8,128)(2,1)} %get-tuple-element.200), channel_id=1, source_target_pairs={{0,24},{8,0},{16,8},{24,16},{1,25},{9,1},{17,9},{25,17},{2,26},{10... | collective-permute-start | bytes 1572872 | tf_op jit(solution)/shard_map/ppermute | solution.py:165
  85.5 327.8 %all-gather.10.cloned.1.call-start = ((), (), s32[]{:S(2)}) async-start(), calls=%async_computation.11 | async-start | bytes 5242880 | tf_op jit(solution)/shard_map/all_gather | solution.py:342
  126.1 34.1 %collective-permute-start.4 = (bf16[128,2048]{1,0:T(8,128)(2,1)S(1)}, bf16[128,2048]{1,0:T(8,128)(2,1)S(1)}, u32[]{:S(2)}, u32[]{:S(2)}) collective-permute-start(bf16[128,2048]{1,0:T(8,128)(2,1)S(1)} %collective-permute-done.2), channel_id=1, source_target_pairs={{0,8},{8,16},{16,24},{24,0},{1,9},{9,17},{17,25},{25,1},{2,10},{10... | collective-permute-start | bytes 1572872 | tf_op jit(solution)/shard_map/ppermute | solution.py:164
  136.0 45.5 %collective-permute-start.5 = (bf16[128,2048]{1,0:T(8,128)(2,1)S(1)}, bf16[128,2048]{1,0:T(8,128)(2,1)S(1)}, u32[]{:S(2)}, u32[]{:S(2)}) collective-permute-start(bf16[128,2048]{1,0:T(8,128)(2,1)S(1)} %collective-permute-done.3), channel_id=1, source_target_pairs={{0,24},{8,0},{16,8},{24,16},{1,25},{9,1},{17,9},{25,17},{2,26},{10... | collective-permute-start | bytes 1572872 | tf_op jit(solution)/shard_map/ppermute | solution.py:165
  191.6 714.1 %reduce-scatter.9.cloned.1.call-start = ((), (), s32[]{:S(2)}) async-start(), calls=%async_computation.14 | async-start | bytes 5242880 | tf_op jit(solution)/shard_map/reduce_scatter | solution.py:413
  241.6 49.3 %collective-permute-start.9 = (bf16[128,2048]{1,0:T(8,128)(2,1)S(1)}, bf16[128,2048]{1,0:T(8,128)(2,1)S(1)}, u32[]{:S(2)}, u32[]{:S(2)}) collective-permute-start(bf16[128,2048]{1,0:T(8,128)(2,1)S(1)} %get-tuple-element.148), channel_id=1, source_target_pairs={{0,24},{8,0},{16,8},{24,16},{1,25},{9,1},{17,9},{25,17},{2,26},{10... | collective-permute-start | bytes 1572872 | tf_op jit(solution)/shard_map/ppermute | solution.py:174
  291.3 49.8 %collective-permute-start.10 = (bf16[128,2048]{1,0:T(8,128)(2,1)S(1)}, bf16[128,2048]{1,0:T(8,128)(2,1)S(1)}, u32[]{:S(2)}, u32[]{:S(2)}) collective-permute-start(bf16[128,2048]{1,0:T(8,128)(2,1)S(1)} %get-tuple-element.146), channel_id=1, source_target_pairs={{0,24},{8,0},{16,8},{24,16},{1,25},{9,1},{17,9},{25,17},{2,26},{10... | collective-permute-start | bytes 1572872 | tf_op jit(solution)/shard_map/ppermute | solution.py:174
  341.5 31.2 %collective-permute-start.11 = (bf16[128,2048]{1,0:T(8,128)(2,1)S(1)}, bf16[128,2048]{1,0:T(8,128)(2,1)S(1)}, u32[]{:S(2)}, u32[]{:S(2)}) collective-permute-start(bf16[128,2048]{1,0:T(8,128)(2,1)S(1)} %get-tuple-element.144), channel_id=1, source_target_pairs={{0,24},{8,0},{16,8},{24,16},{1,25},{9,1},{17,9},{25,17},{2,26},{10... | collective-permute-start | bytes 1572872 | tf_op jit(solution)/shard_map/ppermute | solution.py:174
  417.3 56.7 %collective-permute-start.13 = (bf16[256,2048]{1,0:T(8,128)(2,1)S(1)}, bf16[256,2048]{1,0:T(8,128)(2,1)S(1)}, u32[]{:S(2)}, u32[]{:S(2)}) collective-permute-start(bf16[256,2048]{1,0:T(8,128)(2,1)S(1)} %convolution_convert_fusion.22), channel_id=1, source_target_pairs={{0,1},{1,0},{2,3},{3,2},{4,5},{5,4},{6,7},{7,6},{8,9},{9,8},{10,11... | collective-permute-start | bytes 3145736 | tf_op jit(solution)/shard_map/ppermute | solution.py:183
  527.1 75.2 %collective-permute-start.29 = (bf16[256,2048]{1,0:T(8,128)(2,1)}, bf16[256,2048]{1,0:T(8,128)(2,1)}, u32[]{:S(2)}, u32[]{:S(2)}) collective-permute-start(bf16[256,2048]{1,0:T(8,128)(2,1)} %convolution_convert_fusion.14), channel_id=1, source_target_pairs={{0,1},{1,0},{2,3},{3,2},{4,5},{5,4},{6,7},{7,6},{8,9},{9,8},{10,11... | collective-permute-start | bytes 3145736 | tf_op jit(solution)/shard_map/ppermute | solution.py:183
  549.5 31.3 %collective-permute-start.32 = (bf16[256,2048]{1,0:T(8,128)(2,1)}, bf16[256,2048]{1,0:T(8,128)(2,1)}, u32[]{:S(2)}, u32[]{:S(2)}) collective-permute-start(bf16[256,2048]{1,0:T(8,128)(2,1)} %convolution_convert_fusion.12), channel_id=1, source_target_pairs={{0,1},{1,0},{2,3},{3,2},{4,5},{5,4},{6,7},{7,6},{8,9},{9,8},{10,11... | collective-permute-start | bytes 3145736 | tf_op jit(solution)/shard_map/ppermute | solution.py:183
  570.0 345.8 %reduce-scatter.11.cloned.1.call-start = ((), (), s32[]{:S(2)}) async-start(), calls=%async_computation.15 | async-start | bytes 5242880 | tf_op jit(solution)/shard_map/reduce_scatter | solution.py:413
  631.5 35.6 %collective-permute-start.45 = (bf16[128,2048]{1,0:T(8,128)(2,1)}, bf16[128,2048]{1,0:T(8,128)(2,1)}, u32[]{:S(2)}, u32[]{:S(2)}) collective-permute-start(bf16[128,2048]{1,0:T(8,128)(2,1)} %get-tuple-element.184), channel_id=1, source_target_pairs={{0,24},{8,0},{16,8},{24,16},{1,25},{9,1},{17,9},{25,17},{2,26},{10... | collective-permute-start | bytes 1572872 | tf_op jit(solution)/shard_map/ppermute | solution.py:165
  645.2 301.5 %reduce-scatter.5.cloned.1.call-start = ((), (), s32[]{:S(2)}) async-start(), calls=%async_computation.12 | async-start | bytes 7077888 | tf_op jit(solution)/shard_map/reduce_scatter | solution.py:470
  658.3 29.1 %collective-permute-start.46 = (bf16[128,2048]{1,0:T(8,128)(2,1)}, bf16[128,2048]{1,0:T(8,128)(2,1)}, u32[]{:S(2)}, u32[]{:S(2)}) collective-permute-start(bf16[128,2048]{1,0:T(8,128)(2,1)} %collective-permute-done.44), channel_id=1, source_target_pairs={{0,8},{8,16},{16,24},{24,0},{1,9},{9,17},{17,25},{25,1},{2,10},{10... | collective-permute-start | bytes 1572872 | tf_op jit(solution)/shard_map/ppermute | solution.py:164
  670.4 50.4 %collective-permute-start.47 = (bf16[128,2048]{1,0:T(8,128)(2,1)}, bf16[128,2048]{1,0:T(8,128)(2,1)S(1)}, u32[]{:S(2)}, u32[]{:S(2)}) collective-permute-start(bf16[128,2048]{1,0:T(8,128)(2,1)} %collective-permute-done.45), channel_id=1, source_target_pairs={{0,24},{8,0},{16,8},{24,16},{1,25},{9,1},{17,9},{25,17},{2,26},{10... | collective-permute-start | bytes 1572872 | tf_op jit(solution)/shard_map/ppermute | solution.py:165
  687.5 44.9 %collective-permute-start.48 = (bf16[128,2048]{1,0:T(8,128)(2,1)}, bf16[128,2048]{1,0:T(8,128)(2,1)S(1)}, u32[]{:S(2)}, u32[]{:S(2)}) collective-permute-start(bf16[128,2048]{1,0:T(8,128)(2,1)} %collective-permute-done.46), channel_id=1, source_target_pairs={{0,8},{8,16},{16,24},{24,0},{1,9},{9,17},{17,25},{25,1},{2,10},{10... | collective-permute-start | bytes 1572872 | tf_op jit(solution)/shard_map/ppermute | solution.py:164
  720.8 38.7 %collective-permute-start.49 = (bf16[128,2048]{1,0:T(8,128)(2,1)S(1)}, bf16[128,2048]{1,0:T(8,128)(2,1)S(1)}, u32[]{:S(2)}, u32[]{:S(2)}) collective-permute-start(bf16[128,2048]{1,0:T(8,128)(2,1)S(1)} %collective-permute-done.47), channel_id=1, source_target_pairs={{0,24},{8,0},{16,8},{24,16},{1,25},{9,1},{17,9},{25,17},{2,26},{10... | collective-permute-start | bytes 1572872 | tf_op jit(solution)/shard_map/ppermute | solution.py:165
  789.8 185.9 %reduce-scatter.7.cloned.1.call-start = ((), (), s32[]{:S(2)}) async-start(), calls=%async_computation.13 | async-start | bytes 2359296 | tf_op jit(solution)/shard_map/reduce_scatter | solution.py:482
  (156 other events, 2566.3 us)
Sparse Core Ops, SparseCore 0:
  35.7 59.3 all-gather.11
  97.0 28.9 all-gather.5
  128.1 98.9 all-gather.7
  228.5 139.8 all-gather.9
  570.1 92.9 reduce-scatter.8
  665.8 117.2 reduce-scatter.10
  789.9 59.8 reduce-scatter.4
  869.6 39.2 reduce-scatter.6
